TPU v7x, 32 devices: a whole 2x2x4 slice. The times are simulated.
32 devices in a mesh: user: 8 (over z, x), item: 4 (over y, core).
Axes of the slice: x: 2, y: 2, z: 4, core: 2. Of those that a mesh axis runs over, the one named last changes fastest.
Arguments:
- ratings: bfloat16 [32768, 8192], P('user', 'item'), may hold values from -6 to 6
- tile_mask: int32 [128, 32], P('user', 'item'), may hold values 0 or 1
- user_factors: bfloat16 [128, 256, 128], P('user', 'item'), may hold values from -1.796875 to 1.796875
- item_factors: bfloat16 [8192, 128], P('item'), may hold values from -1.796875 to 1.796875
- neighbours: int32 [128, 4], replicated, may hold values from 0 to 127, as said below
- edge_weight: float32 [128, 4], replicated, may hold values from 0.5 to 8
- dual: float32 [128, 4, 256, 128], P('user', None, 'item'), may hold values from -1.8 to 1.8
Outputs:
- user_update: float32 [128, 256, 128], P('user', 'item')
- dual_update: float32 [128, 4, 256, 128], P('user', None, 'item')
- item_gradient: float32 [8192, 128], P('item')
Inputs may be any that keep to these rules, and one draw needn't show every extreme that they name: `neighbours`: among the 64 entries of rows d * 16 to (d + 1) * 16 - 1, for any d, at most 16 name blocks of one group c * 16 to (c + 1) * 16 - 1, and some group is named exactly 16 times.
All inputs are finite; a program needn't handle non-finite values. No bound on the sum of `tile_mask` on one device may be relied on, other than what follows from the above.
Results may differ from a plain program's by a relative error of at most 0.0012.
Values may be sent and summed in bfloat16 or wider, within the bound.
A program may use at most 128 MiB of HBM per device.

v0:
```python
import math

import jax
import jax.numpy as jnp
from jax import lax
from jax.sharding import PartitionSpec as P

ITERS = 2


descent = 0.5
dual_step = 0.5
primal_step = 0.25


def shards(ratings, tile_mask, user_factors, item_factors, neighbours, edge_weight, dual):
    blocks_here, sub_rows, width = user_factors.shape
    degree = neighbours.shape[1]
    user_count = lax.axis_size("user")
    item_count = lax.axis_size("item")
    item_cols = item_factors.shape[0]
    tile_cols = item_cols // tile_mask.shape[1]
    observed = jnp.repeat(tile_mask.astype(jnp.float32), tile_cols, axis=1)[:, None, :]
    rating_rows = ratings.reshape(blocks_here, sub_rows * item_count, item_cols)
    piece = lax.all_gather(user_factors, "item", axis=1, tiled=True)
    scores = jnp.einsum("bmr,ir->bmi", piece, item_factors, preferred_element_type=jnp.float32)
    errors = (observed * (scores - rating_rows.astype(jnp.float32))).astype(jnp.bfloat16)
    user_term = jnp.einsum("bmi,ir->bmr", errors, item_factors, preferred_element_type=jnp.float32)
    item_term = jnp.einsum("bmi,bmr->ir", errors, piece, preferred_element_type=jnp.float32)
    total_users = blocks_here * sub_rows * item_count * user_count
    total_items = item_cols * item_count
    user_grad = lax.psum_scatter(user_term, "item", scatter_dimension=1, tiled=True) / math.sqrt(
        total_items
    )
    item_grad = lax.psum(item_term, "user")
    item_grad = item_grad / math.sqrt(total_users)
    target = user_factors.astype(jnp.float32) - descent * user_grad
    device_index = lax.axis_index("user")
    edges_here = blocks_here * degree
    total_blocks = blocks_here * user_count
    mine_edges = lax.dynamic_slice_in_dim(
        neighbours, device_index * blocks_here, blocks_here, 0
    ).reshape(-1)
    own_weight = lax.dynamic_slice_in_dim(edge_weight, device_index * blocks_here, blocks_here, 0)
    radius = own_weight.reshape(-1)[:, None]
    primal = target
    extra = target
    flux = dual.reshape(edges_here, sub_rows, width)
    for sweep in range(ITERS):
        gathered = lax.all_gather(extra, "user", axis=0, tiled=True)
        moved = flux + dual_step * (jnp.repeat(extra, degree, axis=0) - gathered[mine_edges])
        length = jnp.sqrt(jnp.sum(moved * moved, axis=-1))
        flux = moved * (radius / jnp.maximum(length, radius))[..., None]
        flat_flux = flux.reshape(edges_here, sub_rows * width)
        chooser = (mine_edges[None, :] == jnp.arange(total_blocks)[:, None]).astype(jnp.float32)
        summed = lax.psum_scatter(
            jnp.dot(
                chooser,
                flat_flux,
                precision=lax.Precision.HIGHEST,
                preferred_element_type=jnp.float32,
            ),
            "user",
            scatter_dimension=0,
            tiled=True,
        )
        divergence = jnp.sum(
            flux.reshape(blocks_here, degree, sub_rows, width), axis=1
        ) - summed.reshape(blocks_here, sub_rows, width)
        newer = (primal - primal_step * divergence + primal_step * target) / (1.0 + primal_step)
        extra = 2.0 * newer - primal
        primal = newer
    return (primal, flux.reshape(blocks_here, degree, sub_rows, width), item_grad)


def solution(mesh):
    in_specs = (
        P("user", "item"),
        P("user", "item"),
        P("user", "item", None),
        P("item", None),
        P(),
        P(),
        P("user", None, "item", None),
    )
    out_specs = (P("user", "item", None), P("user", None, "item", None), P("item", None))
    return jax.shard_map(shards, mesh=mesh, in_specs=in_specs, out_specs=out_specs, check_vma=False)
```

profile of v0, /device:TPU:0, one launch (start us, length us, event | category | flops | bytes accessed | tf_op | source)
XLA Modules:
  0.0 525.6 jit_solution(10700002713590894879)
XLA Ops:
  7.2 0.0 copy-start
  7.2 0.0 all-gather.4.cloned.1.call-start
  7.2 0.7 all-gather.4.cloned.1.call-update
  7.9 0.0 reduce-scatter.4.cloned.1.call-start
  8.0 0.7 convert_element_type.18
  8.7 0.1 copy.22
  8.7 0.1 broadcast_in_dim.6
  8.9 20.2 %all-gather.4.cloned.1.call-done = bf16[16,256,128]{2,1,0:T(8,128)(2,1)} async-done(((bf16[16,64,128]{2,1,0:T(8,128)(2,1)}), bf16[16,256,128]{2,1,0:T(8,128)(2,1)}) %all-gather.4.cloned.1.call-update) | async-done | bytes 1048592 | tf_op jit(solution)/shard_map/all_gather | solution.py:25
  29.0 11.7 %fusion.1 = bf16[16,256,2048]{2,1,0:T(8,128)(2,1)} fusion(bf16[16,256,2048]{2,1,0:T(8,128)(2,1)} %bitcast.93, bf16[16,256,128]{2,1,0:T(8,128)(2,1)} %all-gather.4.cloned.1.call-done, f32[16,2048]{1,0:T(8,128)S(1)} %bitcast.99, bf16[2048,128]{1,0:T(8,128)(2,1)S(1)} %copy-done), kind=kOutput, calls=%fused_computation.4 | convolution fusion | flops 2181038080 | bytes 35258368 | tf_op jit(solution)/shard_map/bmr,ir->bmi/dot_general | solution.py:26
  40.8 9.4 %fusion.20 = f32[16,256,128]{2,1,0:T(8,128)} fusion(bf16[16,256,2048]{2,1,0:T(8,128)(2,1)} %fusion.1, bf16[2048,128]{1,0:T(8,128)(2,1)S(1)} %copy-done), kind=kOutput, calls=%fused_computation.35 | convolution fusion | flops 2147483648 | bytes 19398656 | tf_op jit(solution)/shard_map/bmi,ir->bmr/dot_general | solution.py:28
  50.2 0.0 reduce-scatter.4.cloned.1.call-update
  50.2 0.0 all-gather.6.cloned.1.call-start
  50.3 31.5 %reduce-scatter.4.cloned.1.call-done = f32[16,64,128]{2,1,0:T(8,128)} async-done(((f32[16,256,128]{2,1,0:T(8,128)}), f32[16,64,128]{2,1,0:T(8,128)}) %reduce-scatter.4.cloned.1.call-update) | async-done | bytes 524304 | tf_op jit(solution)/shard_map/reduce_scatter | solution.py:32
  81.8 1.9 multiply_subtract_fusion.1
  83.7 0.0 all-gather.6.cloned.1.call-update
  83.7 0.2 reduce-scatter.6.cloned.1.call-start
  84.0 0.1 constant_dynamic-slice_fusion.1
  84.1 0.1 copy.23
  84.2 0.1 eq.8
  84.2 0.1 reshape.192
  84.3 0.1 constant_dynamic-slice_fusion
  84.4 0.1 copy.24
  84.5 0.1 div.48
  84.6 0.0 copy-start.7
  84.6 73.5 %all-gather.6.cloned.1.call-done = f32[128,64,128]{2,1,0:T(8,128)} async-done(((f32[16,64,128]{2,1,0:T(8,128)}), f32[128,64,128]{2,1,0:T(8,128)}) %all-gather.6.cloned.1.call-update) | async-done | bytes 4194320 | tf_op jit(solution)/shard_map/all_gather | solution.py:50
  158.2 4.2 gather_fusion
  162.4 2.8 multiply_reduce_fusion.1
  165.2 0.1 fusion.30
  165.3 0.1 maximum_divide_fusion.2
  165.4 0.2 broadcast_in_dim.7
  165.7 0.6 mul.109
  166.3 0.7 copy-done.6
  167.0 0.6 copy-done.9
  167.6 7.6 %bitcast_multiply_fusion.2 = f32[64,8192]{1,0:T(8,128)S(1)} fusion(f32[8,8,64,128]{3,2,1,0:T(8,128)S(1)} %bitcast.98, f32[8,8,64,128]{3,2,1,0:T(8,128)S(1)} %bitcast.92, f32[8,8,64,128]{3,2,1,0:T(8,128)S(1)} %bitcast.95, f32[8,8,64,128]{3,2,1,0:T(8,128)S(1)} %bitcast.96), kind=kLoop, calls=%fused_computation.15 | loop fusion | flops 2097152 | bytes 10485760 | tf_op jit(solution)/shard_map/mul | solution.py:53
  175.2 1.3 copy-done.4
  176.5 3.8 fusion.23
  180.3 0.0 reduce-scatter.6.cloned.1.call-update
  180.3 0.3 all-gather.8.cloned.1.call-start
  180.6 1.5 multiply_reduce_fusion.2
  182.1 84.5 %reduce-scatter.6.cloned.1.call-done = f32[16,8192]{1,0:T(8,128)} async-done(((f32[128,8192]{1,0:T(8,128)}), f32[16,8192]{1,0:T(8,128)}) %reduce-scatter.6.cloned.1.call-update) | async-done | bytes 524304 | tf_op jit(solution)/shard_map/reduce_scatter | solution.py:56
  266.6 1.1 copy.34
  267.8 2.2 multiply_subtract_fusion
  270.0 0.0 all-gather.8.cloned.1.call-update
  270.0 0.0 all-reduce.2.cloned.1.call-start
  270.0 11.6 %convolution_bitcast_fusion = f32[2048,128]{1,0:T(8,128)} fusion(bf16[16,256,2048]{2,1,0:T(8,128)(2,1)} %fusion.1, bf16[16,256,128]{2,1,0:T(8,128)(2,1)} %all-gather.4.cloned.1.call-done), kind=kOutput, calls=%fused_computation.5 | convolution fusion | flops 2147483648 | bytes 18874368 | tf_op jit(solution)/shard_map/bmi,bmr->ir/dot_general | solution.py:29
  281.6 0.0 all-reduce.2.cloned.1.call-update
  281.7 0.0 reduce-scatter.8.cloned.1.call-start
  281.7 61.6 %all-gather.8.cloned.1.call-done = f32[128,64,128]{2,1,0:T(8,128)} async-done(((f32[16,64,128]{2,1,0:T(8,128)}), f32[128,64,128]{2,1,0:T(8,128)}) %all-gather.8.cloned.1.call-update) | async-done | bytes 4194320 | tf_op jit(solution)/shard_map/all_gather | solution.py:50
  343.3 4.2 gather_fusion.1
  347.5 2.5 multiply_reduce_fusion
  350.0 0.1 fusion.29
  350.1 0.1 maximum_divide_fusion
  350.2 0.2 broadcast_in_dim.8
  350.5 0.6 mul.121
  351.1 0.9 copy-done.2
  352.0 0.6 copy-done.5
  352.6 8.4 %fusion.2 = f32[128,8192]{1,0:T(8,128)} fusion(f32[8,8,64,128]{3,2,1,0:T(8,128)S(1)} %bitcast.97, f32[64,8192]{1,0:T(8,128)S(1)} %copy-done.5, f32[8,8,64,128]{3,2,1,0:T(8,128)S(1)} %bitcast.90, f32[8,8,64,128]{3,2,1,0:T(8,128)S(1)} %bitcast.94, s32[64]{0:T(128)S(1)} %eq.8), kind=kOutput, calls=%fused_computation.7 | convolution fusion | flops 807411712 | bytes 12583168 | tf_op jit(solution)/shard_map/dot_general | solution.py:57
  361.0 0.0 reduce-scatter.8.cloned.1.call-update
  361.0 62.5 %all-reduce.2.cloned.1.call-done = f32[2048,128]{1,0:T(8,128)} async-done(((f32[2048,128]{1,0:T(8,128)}), f32[2048,128]{1,0:T(8,128)}) %all-reduce.2.cloned.1.call-update) | async-done | bytes 1048592 | tf_op jit(solution)/shard_map/psum | solution.py:35
  423.5 2.4 broadcast_multiply_fusion.1
  426.0 3.0 fusion.28
  429.0 86.1 %reduce-scatter.8.cloned.1.call-done = f32[16,8192]{1,0:T(8,128)} async-done(((f32[128,8192]{1,0:T(8,128)}), f32[16,8192]{1,0:T(8,128)}) %reduce-scatter.8.cloned.1.call-update) | async-done | bytes 524304 | tf_op jit(solution)/shard_map/reduce_scatter | solution.py:56
  515.2 1.2 copy.38
  516.4 2.4 fusion.16
  (24 shorter events, 0.1 us)
Async XLA Ops:
  7.2 21.9 %copy-start = (bf16[2048,128]{1,0:T(8,128)(2,1)S(1)}, bf16[2048,128]{1,0:T(8,128)(2,1)}, u32[]{:S(2)}) copy-start(bf16[2048,128]{1,0:T(8,128)(2,1)} %param.10) | copy-start | bytes 1572868
  7.2 21.9 %all-gather.4.cloned.1.call-start = ((), (), s32[]{:S(2)}) async-start(), calls=%async_computation.3 | async-start | bytes 1310720 | tf_op jit(solution)/shard_map/all_gather | solution.py:25
  7.9 73.9 %reduce-scatter.4.cloned.1.call-start = ((), (), s32[]{:S(2)}) async-start(), calls=%async_computation.4 | async-start | bytes 2621440 | tf_op jit(solution)/shard_map/reduce_scatter | solution.py:32
  50.2 31.6 %copy-start.11 = (bf16[16,64,128]{2,1,0:T(8,128)(2,1)S(1)}, bf16[16,64,128]{2,1,0:T(8,128)(2,1)}, u32[]{:S(2)}) copy-start(bf16[16,64,128]{2,1,0:T(8,128)(2,1)} %param.9) | copy-start | bytes 786436
  50.2 33.8 %copy-start.12 = (s32[128,4]{0,1:T(4,128)S(1)}, s32[128,4]{0,1:T(4,128)}, u32[]{:S(2)}) copy-start(s32[128,4]{0,1:T(4,128)} %param.11) | copy-start | bytes 6148
  50.2 34.1 %copy-start.13 = (f32[128,4]{0,1:T(4,128)S(1)}, f32[128,4]{0,1:T(4,128)}, u32[]{:S(2)}) copy-start(f32[128,4]{0,1:T(4,128)} %param.12) | copy-start | bytes 6148
  50.2 107.9 %all-gather.6.cloned.1.call-start = ((), (), s32[]{:S(2)}) async-start(), calls=%async_computation.5 | async-start | bytes 4718592 | tf_op jit(solution)/shard_map/all_gather | solution.py:50
  83.7 182.9 %reduce-scatter.6.cloned.1.call-start = ((), (), s32[]{:S(2)}) async-start(), calls=%async_computation.6 | async-start | bytes 4718592 | tf_op jit(solution)/shard_map/reduce_scatter | solution.py:56
  84.6 77.7 %copy-start.7 = (f32[16,64,128]{2,1,0:T(8,128)S(1)}, f32[16,64,128]{2,1,0:T(8,128)}, u32[]{:S(2)}) copy-start(f32[16,64,128]{2,1,0:T(8,128)} %multiply_subtract_fusion.1) | copy-start | bytes 1572868
  165.4 1.6 copy-start.6
  165.4 2.2 copy-start.9
  175.2 1.3 copy-start.4
  180.3 163.0 %all-gather.8.cloned.1.call-start = ((), (), s32[]{:S(2)}) async-start(), calls=%async_computation.7 | async-start | bytes 4718592 | tf_op jit(solution)/shard_map/all_gather | solution.py:50
  267.8 13.9 %copy-start.10 = (f32[2,8,64,128]{3,2,1,0:T(8,128)}, f32[2,8,64,128]{3,2,1,0:T(8,128)S(1)}, u32[]{:S(2)}) copy-start(f32[2,8,64,128]{3,2,1,0:T(8,128)S(1)} %copy.34) | copy-start | bytes 1572868
  270.0 153.6 %all-reduce.2.cloned.1.call-start = ((), (), s32[]{:S(2)}) async-start(), calls=%async_computation.9 | async-start | bytes 2097152 | tf_op jit(solution)/shard_map/psum | solution.py:35
  281.7 65.8 %copy-start.8 = (f32[16,64,128]{2,1,0:T(8,128)S(1)}, f32[16,64,128]{2,1,0:T(8,128)}, u32[]{:S(2)}) copy-start(f32[16,64,128]{2,1,0:T(8,128)} %multiply_subtract_fusion) | copy-start | bytes 1572868
  281.7 233.5 %reduce-scatter.8.cloned.1.call-start = ((), (), s32[]{:S(2)}) async-start(), calls=%async_computation.8 | async-start | bytes 4718592 | tf_op jit(solution)/shard_map/reduce_scatter | solution.py:56
  350.2 1.8 copy-start.2
  350.2 2.4 copy-start.5
  423.5 2.4 copy-start.3
  515.2 3.6 copy-start.1
Sparse Core Ops, SparseCore 0:
  9.6 19.4 all-gather.3
  50.4 31.4 reduce-scatter.3
  84.7 73.3 all-gather.5
  180.4 86.1 reduce-scatter.5
  270.1 73.1 all-gather.7
  347.2 76.2 all-reduce.1
  427.6 87.5 reduce-scatter.7
where the time goes:
time: 526 us
  waiting for transfers between devices  421 us (80%)
  matrix products  44.9 us (9%)
  other arithmetic  27.5 us (5%)
  local copies, waits for them, and re-layouts  17.5 us (3%)
  between operations  14.3 us (3%)
    reduce_scatter x2, waiting for transfers between devices, shards(): lax.psum_scatter(jnp.dot(chooser, flat_flux, precision=lax.Precision.HIGH...  171 us
    all_gather x2, waiting for transfers between devices, shards(): gathered = lax.all_gather(extra, 'user', axis=0, tiled=True)  135 us
    psum x1, waiting for transfers between devices, shards(): item_grad = lax.psum(item_term, 'user')  62.5 us
    reduce_scatter x1, waiting for transfers between devices, shards(): lax.psum_scatter(user_term, 'item', scatter_dimension=1, tiled=True)  31.5 us
    all_gather x1, waiting for transfers between devices, shards(): piece = lax.all_gather(user_factors, 'item', axis=1, tiled=True)  20.2 us
    dot_general x2, matrix products, shards(): jnp.dot(chooser, flat_flux, precision=lax.Precision.HIGHEST, preferred_el...  12.1 us
    dot_general x1, matrix products, shards(): jnp.einsum('bmr,ir->bmi', piece, item_factors, preferred_element_type=jnp...  11.7 us
    dot_general x1, matrix products, shards(): jnp.einsum('bmi,bmr->ir', errors, piece, preferred_element_type=jnp.float32)  11.6 us
  transfers between devices with their start and end apart: 7, of which 7 were waited for; matrix products, arithmetic and copies ran while one was open for 7% of the time, Pallas kernels for 0%

commit v1 on v0

v1 whole, which is shorter than its diff:
```python
import functools
import math

import jax
import jax.numpy as jnp
from jax import lax
from jax.experimental import pallas as pl
from jax.experimental.pallas import tpu as pltpu
from jax.sharding import PartitionSpec as P

ITERS = 2

descent = 0.5
dual_step = 0.5
primal_step = 0.25


def gradient_kernel(tiles, mask_ref, piece_ref, rating_ref, item_ref, user_out, item_out):
    b = pl.program_id(0)
    width = item_ref.shape[0] // tiles

    @pl.when(b == 0)
    def _():
        item_out[...] = jnp.zeros_like(item_out)

    user_out[...] = jnp.zeros_like(user_out)
    for t in range(tiles):

        @pl.when(mask_ref[b, t] != 0)
        def _():
            cols = pl.ds(t * width, width)
            users = piece_ref[0]
            items = item_ref[cols, :]
            scores = lax.dot_general(
                users, items, (((1,), (1,)), ((), ())), preferred_element_type=jnp.float32
            )
            errors = (scores - rating_ref[:, cols].astype(jnp.float32)).astype(jnp.bfloat16)
            user_out[0] += jnp.dot(errors, items, preferred_element_type=jnp.float32)
            item_out[cols, :] += lax.dot_general(
                errors, users, (((0,), (0,)), ((), ())), preferred_element_type=jnp.float32
            )


def gradients(tile_mask, piece, ratings, item_factors):
    blocks, rows, width = piece.shape
    cols = item_factors.shape[0]
    tiles = tile_mask.shape[1]
    return pl.pallas_call(
        functools.partial(gradient_kernel, tiles),
        out_shape=(
            jax.ShapeDtypeStruct((blocks, rows, width), jnp.float32),
            jax.ShapeDtypeStruct((cols, width), jnp.float32),
        ),
        grid_spec=pltpu.PrefetchScalarGridSpec(
            num_scalar_prefetch=1,
            grid=(blocks,),
            in_specs=[
                pl.BlockSpec((1, rows, width), lambda b, m: (b, 0, 0)),
                pl.BlockSpec((rows, cols), lambda b, m: (b, 0)),
                pl.BlockSpec((cols, width), lambda b, m: (0, 0)),
            ],
            out_specs=[
                pl.BlockSpec((1, rows, width), lambda b, m: (b, 0, 0)),
                pl.BlockSpec((cols, width), lambda b, m: (0, 0)),
            ],
        ),
        compiler_params=pltpu.CompilerParams(vmem_limit_bytes=32 << 20),
        cost_estimate=pl.CostEstimate(
            flops=6 * blocks * rows * cols * width,
            bytes_accessed=2 * blocks * rows * cols,
            transcendentals=0,
        ),
    )(tile_mask, piece, ratings, item_factors)


def variation_kernel(group, near_ref, weight_ref, target_ref, dual_ref, out_ref, extra_ref, div_ref):
    blocks, degree = dual_ref.shape[:2]

    for sweep in range(ITERS):
        source = target_ref if sweep == 0 else extra_ref
        div_ref[...] = jnp.zeros_like(div_ref)

        def edges(step, _):
            first = step * group
            todo = []
            for j in range(group):
                a = first + j
                here = source[a]
                total = None
                for k in range(degree):
                    e = a * degree + k
                    to = near_ref[e]
                    w = weight_ref[e]
                    flux = dual_ref[a, k] if sweep == 0 else out_ref[a, k]
                    moved = flux + dual_step * (here - source[to])
                    square = jnp.sum(moved * moved, axis=-1, keepdims=True)
                    flux = moved * (w * lax.rsqrt(jnp.maximum(square, w * w)))
                    out_ref[a, k] = flux
                    total = flux if total is None else total + flux
                    todo.append((to, -flux))
                todo.append((a, total))
            for place, term in todo:
                div_ref[place] += term
            return 0

        lax.fori_loop(0, blocks // group, edges, 0)

        target = target_ref[...]
        primal = target if sweep == 0 else out_ref[:, degree]
        newer = (primal - primal_step * div_ref[...] + primal_step * target) / (1.0 + primal_step)
        if sweep < ITERS - 1:
            extra_ref[...] = 2.0 * newer - primal
        out_ref[:, degree] = newer


def variation(near, weight, target, dual):
    blocks, degree, rows, width = dual.shape
    group = next(g for g in (4, 2, 1) if blocks % g == 0)
    vmem = pl.BlockSpec(memory_space=pltpu.VMEM)
    smem = pl.BlockSpec(memory_space=pltpu.SMEM)
    return pl.pallas_call(
        functools.partial(variation_kernel, group),
        out_shape=jax.ShapeDtypeStruct((blocks, degree + 1, rows, width), jnp.float32),
        in_specs=[smem, smem, vmem, vmem],
        out_specs=vmem,
        scratch_shapes=[
            pltpu.VMEM((blocks, rows, width), jnp.float32),
            pltpu.VMEM((blocks, rows, width), jnp.float32),
        ],
        compiler_params=pltpu.CompilerParams(vmem_limit_bytes=32 << 20),
        cost_estimate=pl.CostEstimate(
            flops=20 * ITERS * dual.size, bytes_accessed=8 * dual.size, transcendentals=0
        ),
    )(near.reshape(-1), weight.reshape(-1), target, dual)


def shards(ratings, tile_mask, user_factors, item_factors, neighbours, edge_weight, dual):
    blocks_here, sub_rows, width = user_factors.shape
    degree = neighbours.shape[1]
    user_count = lax.axis_size("user")
    item_count = lax.axis_size("item")
    item_cols = item_factors.shape[0]
    thin = sub_rows // user_count
    total_blocks = blocks_here * user_count

    dual_parts = dual.reshape(blocks_here, degree, user_count, thin, width).transpose(2, 0, 1, 3, 4)
    dual_rows = lax.all_to_all(dual_parts, "user", 0, 0, tiled=True).reshape(
        total_blocks, degree, thin, width
    )

    piece = lax.all_gather(user_factors, "item", axis=1, tiled=True)
    user_term, item_term = gradients(tile_mask, piece, ratings, item_factors)
    total_users = blocks_here * sub_rows * item_count * user_count
    total_items = item_cols * item_count
    user_grad = lax.psum_scatter(user_term, "item", scatter_dimension=1, tiled=True) / math.sqrt(
        total_items
    )
    item_grad = lax.psum(item_term, "user") / math.sqrt(total_users)
    target = user_factors.astype(jnp.float32) - descent * user_grad
    target_parts = target.reshape(blocks_here, user_count, thin, width).transpose(1, 0, 2, 3)
    target_rows = lax.all_to_all(target_parts, "user", 0, 0, tiled=True).reshape(
        total_blocks, thin, width
    )
    result = variation(neighbours, edge_weight, target_rows, dual_rows)
    result = result.reshape(user_count, blocks_here, degree + 1, thin, width)
    result = lax.all_to_all(result, "user", 0, 0, tiled=True)
    result = result.transpose(1, 2, 0, 3, 4).reshape(blocks_here, degree + 1, sub_rows, width)
    return (result[:, degree], result[:, :degree], item_grad)


def solution(mesh):
    in_specs = (
        P("user", "item"),
        P("user", "item"),
        P("user", "item", None),
        P("item", None),
        P(),
        P(),
        P("user", None, "item", None),
    )
    out_specs = (P("user", "item", None), P("user", None, "item", None), P("item", None))
    return jax.shard_map(shards, mesh=mesh, in_specs=in_specs, out_specs=out_specs, check_vma=False)
```

time: 526 us -> 294 us (0.56)
  waiting for transfers between devices: 421 us -> 199 us
  matrix products: 44.9 us -> 0 us
  Pallas kernels: 0 us -> 41.5 us
  other arithmetic: 27.5 us -> 4.18 us
  starting transfers between devices: 0.69 us -> 15.8 us
    reduce_scatter x2 -> x0, waiting for transfers between devices: 171 us -> none  [shards(): lax.psum_scatter(jnp.dot(chooser, flat_flux, precision=lax.Precision.HIGH...]
    all_gather x2 -> x0, waiting for transfers between devices: 135 us -> none  [shards(): gathered = lax.all_gather(extra, 'user', axis=0, tiled=True)]
    psum x1, waiting for transfers between devices: 62.5 us -> 120 us  [shards(): item_grad = lax.psum(item_term, 'user') / math.sqrt(total_users)]
    dot_general x5 -> x0, matrix products: 44.9 us -> none  [the longest x2 12.1 us: shards(): jnp.dot(chooser, flat_flux, precision=lax.Precision.HIGHEST, preferred_el...]
    pallas_call x0 -> x2, Pallas kernels: none -> 41.5 us  [the longest x1 30.4 us: gradients(): pl.pallas_call(functools.partial(gradient_kernel, tiles), out_shape=(jax....]
    all_to_all x0 -> x3, waiting for transfers between devices: none -> 32.9 us  [the longest x1 18.8 us: shards(): lax.all_to_all(dual_parts, 'user', 0, 0, tiled=True)]
    all_to_all x0 -> x3, starting transfers between devices: none -> 15.7 us  [the longest x1 7.83 us: shards(): lax.all_to_all(dual_parts, 'user', 0, 0, tiled=True)]
    reduce_sum x4 -> x0, other arithmetic: 9.95 us -> none  [the longest x2 5.38 us: shards(): length = jnp.sqrt(jnp.sum(moved * moved, axis=-1))]
  transfers between devices with their start and end apart: 7 -> 6, of which waited for: 7 -> 5; matrix products, arithmetic and copies ran while one was open for 7% -> 2% of each run, Pallas kernels for 0% -> 0%
where the time goes in v1:
time: 294 us; the launch traced here: 292 us
  waiting for transfers between devices  199 us (68%)
  Pallas kernels  41.5 us (14%)
  local copies, waits for them, and re-layouts  18.1 us (6%)
  starting transfers between devices  15.8 us (5%)
  between operations  13.8 us (5%)
  other arithmetic  4.18 us (1%)
    psum x1, waiting for transfers between devices, shards(): item_grad = lax.psum(item_term, 'user') / math.sqrt(total_users)  120 us
    pallas_call x1, Pallas kernels, gradients(): pl.pallas_call(functools.partial(gradient_kernel, tiles), out_shape=(jax....  30.4 us
    reduce_scatter x1, waiting for transfers between devices, shards(): lax.psum_scatter(user_term, 'item', scatter_dimension=1, tiled=True)  24.6 us
    all_gather x1, waiting for transfers between devices, shards(): piece = lax.all_gather(user_factors, 'item', axis=1, tiled=True)  20.3 us
    all_to_all x1, waiting for transfers between devices, shards(): lax.all_to_all(dual_parts, 'user', 0, 0, tiled=True)  18.8 us
    all_to_all x1, waiting for transfers between devices, shards(): lax.all_to_all(target_parts, 'user', 0, 0, tiled=True)  14.1 us
    unnamed x21, local copies, waits for them, and re-layouts  11.9 us
    pallas_call x1, Pallas kernels, variation(): pl.pallas_call(functools.partial(variation_kernel, group), out_shape=jax....  11.1 us
  transfers between devices with their start and end apart: 6, of which 5 were waited for; matrix products, arithmetic and copies ran while one was open for 2% of the time, Pallas kernels for 0%

profile of v1, /device:TPU:0, one launch (start us, length us, event | category | flops | bytes accessed | tf_op | source)
XLA Modules:
  0.0 292.3 jit_solution(10782962726600050656)
XLA Ops:
  7.2 0.0 copy-start
  7.2 0.0 all-gather.2.cloned.1.call-start
  7.2 0.7 all-gather.2.cloned.1.call-update
  7.9 0.0 reduce-scatter.2.cloned.1.call-start
  8.0 0.8 copy.16.mask_ref
  8.7 20.3 %all-gather.2.cloned.1.call-done.piece_ref = bf16[16,256,128]{2,1,0:T(8,128)(2,1)} async-done(((bf16[16,64,128]{2,1,0:T(8,128)(2,1)}), bf16[16,256,128]{2,1,0:T(8,128)(2,1)}) %all-gather.2.cloned.1.call-update) | async-done | bytes 1048592 | tf_op jit(solution)/shard_map/all_gather | solution.py:151
  29.0 0.0 copy-start.3
  29.0 5.8 %copy-done.3 = bf16[4096,2048]{1,0:T(8,128)(2,1)S(1)} copy-done((bf16[4096,2048]{1,0:T(8,128)(2,1)S(1)}, bf16[4096,2048]{1,0:T(8,128)(2,1)}, u32[]{:S(2)}) %copy-start.3) | copy-done | bytes 16777240
  34.8 0.0 copy-start.4
  34.8 1.2 copy-done.4
  36.0 0.0 copy-start.5
  36.0 1.0 copy-done.5
  37.1 30.4 %shard_map.94 = (f32[16,256,128]{2,1,0:T(8,128)S(1)}, f32[2048,128]{1,0:T(8,128)}) custom-call(s32[16,8]{1,0:T(8,128)S(1)} %copy.16.mask_ref, bf16[16,256,128]{2,1,0:T(8,128)(2,1)S(1)} %copy-done.4, bf16[4096,2048]{1,0:T(8,128)(2,1)S(1)} %copy-done.3, bf16[2048,128]{1,0:T(8,128)(2,1)S(1)} %copy-done.5), custom_call_target="tpu_custom_call" | custom-call | flops 6442450944 | bytes 16777216 | tf_op jit(solution)/shard_map/pallas_call | solution.py:48
  67.4 0.0 copy-start.2
  67.4 1.3 copy-done.2
  68.8 0.0 reduce-scatter.2.cloned.1.call-update
  68.8 0.0 copy-done
  68.8 1.6 copy_bitcast_fusion.1
  70.4 0.0 copy-start.6
  70.4 0.0 copy-start.7
  70.4 0.0 copy-start.8
  70.4 7.8 %all-to-all-start.1 = ((f32[8,16,4,8,128]{4,3,2,1,0:T(8,128)}), f32[8,16,4,8,128]{4,3,2,1,0:T(8,128)}, u32[]{:S(2)}, u32[]{:S(2)}) async-start(f32[8,16,4,8,128]{4,3,2,1,0:T(8,128)} %copy_bitcast_fusion.1), calls=%async_computation.2 | async-start | bytes 4194304 | tf_op jit(solution)/shard_map/all_to_all | solution.py:147
  78.2 24.6 %reduce-scatter.2.cloned.1.call-done = f32[16,64,128]{2,1,0:T(8,128)} async-done(((f32[16,256,128]{2,1,0:T(8,128)}), f32[16,64,128]{2,1,0:T(8,128)}) %reduce-scatter.2.cloned.1.call-update) | async-done | bytes 524304 | tf_op jit(solution)/shard_map/reduce_scatter | solution.py:155
  102.9 0.0 copy-done.6
  102.9 1.9 copy_bitcast_fusion.2
  104.8 18.8 %all-to-all-done.1 = f32[8,16,4,8,128]{4,3,2,1,0:T(8,128)} async-done(((f32[8,16,4,8,128]{4,3,2,1,0:T(8,128)}), f32[8,16,4,8,128]{4,3,2,1,0:T(8,128)}, u32[]{:S(2)}, u32[]{:S(2)}) %all-to-all-start.1) | async-done | bytes 2097184 | tf_op jit(solution)/shard_map/all_to_all | solution.py:147
  123.6 3.5 %all-to-all-start = ((f32[8,16,8,128]{3,2,1,0:T(8,128)}), f32[8,16,8,128]{3,2,1,0:T(8,128)S(1)}, u32[]{:S(2)}, u32[]{:S(2)}) async-start(f32[8,16,8,128]{3,2,1,0:T(8,128)} %copy_bitcast_fusion.2), calls=%async_computation.1 | async-start | bytes 1048576 | tf_op jit(solution)/shard_map/all_to_all | solution.py:161
  127.1 0.0 copy-done.7
  127.1 0.1 copy.14
  127.2 0.1 reshape.30.near_ref
  127.3 0.0 copy-done.8
  127.3 0.1 copy.15
  127.4 0.1 reshape.31.weight_ref
  127.5 14.1 %all-to-all-done = f32[8,16,8,128]{3,2,1,0:T(8,128)S(1)} async-done(((f32[8,16,8,128]{3,2,1,0:T(8,128)}), f32[8,16,8,128]{3,2,1,0:T(8,128)S(1)}, u32[]{:S(2)}, u32[]{:S(2)}) %all-to-all-start) | async-done | bytes 524320 | tf_op jit(solution)/shard_map/all_to_all | solution.py:161
  141.7 11.1 %shard_map.95 = f32[128,5,8,128]{3,2,1,0:T(8,128)S(1)} custom-call(s32[512]{0:T(512)S(1)} %reshape.30.near_ref, f32[512]{0:T(512)S(1)} %reshape.31.weight_ref, f32[128,8,128]{2,1,0:T(8,128)S(1)} %bitcast.21, f32[128,4,8,128]{3,2,1,0:T(8,128)} %bitcast.5.dual_ref), custom_call_target="tpu_custom_call" | custom-call | flops 20971520 | bytes 4194304 | tf_op jit(solution)/shard_map/pallas_call | solution.py:121
  152.8 0.0 copy-start.1
  152.8 1.5 copy-done.1
  154.3 4.4 %all-to-all-start.2 = ((f32[8,16,5,8,128]{4,3,2,1,0:T(8,128)}), f32[8,16,5,8,128]{4,3,2,1,0:T(8,128)}, u32[]{:S(2)}, u32[]{:S(2)}) async-start(f32[8,16,5,8,128]{4,3,2,1,0:T(8,128)} %bitcast.20), calls=%async_computation.3 | async-start | bytes 5242880 | tf_op jit(solution)/shard_map/all_to_all | solution.py:166
  158.7 0.0 all-reduce.2.cloned.1.call-start
  158.7 0.7 all-reduce.2.cloned.1.call-update
  159.4 119.7 %all-reduce.2.cloned.1.call-done = f32[2048,128]{1,0:T(8,128)} async-done(((f32[2048,128]{1,0:T(8,128)}), f32[2048,128]{1,0:T(8,128)}) %all-reduce.2.cloned.1.call-update) | async-done | bytes 1048592 | tf_op jit(solution)/shard_map/psum | solution.py:158
  279.1 2.3 broadcast_multiply_fusion
  281.4 0.0 all-to-all-done.2
  281.4 2.1 copy_bitcast_fusion
  283.5 0.8 slice_bitcast_fusion
  284.3 1.5 slice.9
Async XLA Ops:
  7.2 61.6 %copy-start = (f32[16,4,64,128]{3,2,1,0:T(8,128)S(1)}, f32[16,4,64,128]{3,2,1,0:T(8,128)}, u32[]{:S(2)}) copy-start(f32[16,4,64,128]{3,2,1,0:T(8,128)} %param.13) | copy-start | bytes 6291460
  7.2 21.9 %all-gather.2.cloned.1.call-start = ((), (), s32[]{:S(2)}) async-start(), calls=%async_computation.4 | async-start | bytes 1310720 | tf_op jit(solution)/shard_map/all_gather | solution.py:151
  7.9 95.0 %reduce-scatter.2.cloned.1.call-start = ((), (), s32[]{:S(2)}) async-start(), calls=%async_computation.5 | async-start | bytes 2621440 | tf_op jit(solution)/shard_map/reduce_scatter | solution.py:155
  29.0 5.8 %copy-start.3 = (bf16[4096,2048]{1,0:T(8,128)(2,1)S(1)}, bf16[4096,2048]{1,0:T(8,128)(2,1)}, u32[]{:S(2)}) copy-start(bf16[4096,2048]{1,0:T(8,128)(2,1)} %rating_ref.1) | copy-start | bytes 50331652
  34.8 1.2 copy-start.4
  36.0 1.0 copy-start.5
  67.4 1.3 copy-start.2
  70.4 32.5 %copy-start.6 = (bf16[16,64,128]{2,1,0:T(8,128)(2,1)S(1)}, bf16[16,64,128]{2,1,0:T(8,128)(2,1)}, u32[]{:S(2)}) copy-start(bf16[16,64,128]{2,1,0:T(8,128)(2,1)} %param.9) | copy-start | bytes 786436
  70.4 56.7 %copy-start.7 = (s32[128,4]{0,1:T(4,128)S(1)}, s32[128,4]{0,1:T(4,128)}, u32[]{:S(2)}) copy-start(s32[128,4]{0,1:T(4,128)} %param.11) | copy-start | bytes 6148
  70.4 56.9 %copy-start.8 = (f32[128,4]{0,1:T(4,128)S(1)}, f32[128,4]{0,1:T(4,128)}, u32[]{:S(2)}) copy-start(f32[128,4]{0,1:T(4,128)} %param.12) | copy-start | bytes 6148
  70.4 53.2 %all-to-all-start.1 = ((f32[8,16,4,8,128]{4,3,2,1,0:T(8,128)}), f32[8,16,4,8,128]{4,3,2,1,0:T(8,128)}, u32[]{:S(2)}, u32[]{:S(2)}) async-start(f32[8,16,4,8,128]{4,3,2,1,0:T(8,128)} %copy_bitcast_fusion.1), calls=%async_computation.2 | async-start | bytes 4194304 | tf_op jit(solution)/shard_map/all_to_all | solution.py:147
  123.6 18.1 %all-to-all-start = ((f32[8,16,8,128]{3,2,1,0:T(8,128)}), f32[8,16,8,128]{3,2,1,0:T(8,128)S(1)}, u32[]{:S(2)}, u32[]{:S(2)}) async-start(f32[8,16,8,128]{3,2,1,0:T(8,128)} %copy_bitcast_fusion.2), calls=%async_computation.1 | async-start | bytes 1048576 | tf_op jit(solution)/shard_map/all_to_all | solution.py:161
  152.8 1.5 copy-start.1
  154.3 127.1 %all-to-all-start.2 = ((f32[8,16,5,8,128]{4,3,2,1,0:T(8,128)}), f32[8,16,5,8,128]{4,3,2,1,0:T(8,128)}, u32[]{:S(2)}, u32[]{:S(2)}) async-start(f32[8,16,5,8,128]{4,3,2,1,0:T(8,128)} %bitcast.20), calls=%async_computation.3 | async-start | bytes 5242880 | tf_op jit(solution)/shard_map/all_to_all | solution.py:166
  158.7 120.4 %all-reduce.2.cloned.1.call-start = ((), (), s32[]{:S(2)}) async-start(), calls=%async_computation.6 | async-start | bytes 2097152 | tf_op jit(solution)/shard_map/psum | solution.py:158
Sparse Core Ops, SparseCore 0:
  9.6 19.4 all-gather.1
  68.9 33.9 reduce-scatter.1
  164.0 115.0 all-reduce.1

commit v2 on v1

--- a/solution.py
+++ b/solution.py
@@ -9,46 +9,67 @@
 from jax.sharding import PartitionSpec as P
 
 ITERS = 2
+PAIR = 2
+WIRE = jnp.float16
 
 descent = 0.5
 dual_step = 0.5
 primal_step = 0.25
 
 
-def gradient_kernel(tiles, mask_ref, piece_ref, rating_ref, item_ref, user_out, item_out):
+def gradient_kernel(tiles, mask_ref, piece_ref, rating_ref, item_ref, user_out, item_out, active, total):
     b = pl.program_id(0)
     width = item_ref.shape[0] // tiles
+    parts, _, sub, rank = user_out.shape
 
     @pl.when(b == 0)
     def _():
-        item_out[...] = jnp.zeros_like(item_out)
+        total[...] = jnp.zeros_like(total)
+
+    count = 0
+    for t in range(tiles):
+        active[count] = t
+        count = count + jnp.where(mask_ref[b, t] != 0, 1, 0)
 
     user_out[...] = jnp.zeros_like(user_out)
-    for t in range(tiles):
-
-        @pl.when(mask_ref[b, t] != 0)
-        def _():
-            cols = pl.ds(t * width, width)
-            users = piece_ref[0]
+    users = piece_ref[0]
+    across = users.T
+
+    def pair(step, _):
+        first = step * PAIR
+        user_sum = None
+        for j in range(PAIR):
+            at = jnp.minimum(first + j, count - 1)
+            keep = jnp.where(first + j < count, 1.0, 0.0)
+            cols = pl.ds(pl.multiple_of(active[at] * width, width), width)
             items = item_ref[cols, :]
             scores = lax.dot_general(
                 users, items, (((1,), (1,)), ((), ())), preferred_element_type=jnp.float32
             )
-            errors = (scores - rating_ref[:, cols].astype(jnp.float32)).astype(jnp.bfloat16)
-            user_out[0] += jnp.dot(errors, items, preferred_element_type=jnp.float32)
-            item_out[cols, :] += lax.dot_general(
-                errors, users, (((0,), (0,)), ((), ())), preferred_element_type=jnp.float32
-            )
-
-
-def gradients(tile_mask, piece, ratings, item_factors):
+            errors = (keep * (scores - rating_ref[:, cols].astype(jnp.float32))).astype(jnp.bfloat16)
+            term = jnp.dot(errors, items, preferred_element_type=jnp.float32)
+            user_sum = term if user_sum is None else user_sum + term
+            total[:, cols] += jnp.dot(across, errors, preferred_element_type=jnp.float32)
+        for p in range(parts):
+            user_out[p, 0] += user_sum[p * sub : (p + 1) * sub]
+        return 0
+
+    lax.fori_loop(0, (count + PAIR - 1) // PAIR, pair, 0)
+
+    @pl.when(b == pl.num_programs(0) - 1)
+    def _():
+        item_out[...] = total[...].T
+
+
+def gradients(tile_mask, piece, ratings, item_factors, parts):
     blocks, rows, width = piece.shape
     cols = item_factors.shape[0]
     tiles = tile_mask.shape[1]
+    sub = rows // parts
     return pl.pallas_call(
         functools.partial(gradient_kernel, tiles),
         out_shape=(
-            jax.ShapeDtypeStruct((blocks, rows, width), jnp.float32),
+            jax.ShapeDtypeStruct((parts, blocks, sub, width), jnp.float32),
             jax.ShapeDtypeStruct((cols, width), jnp.float32),
         ),
         grid_spec=pltpu.PrefetchScalarGridSpec(
@@ -60,13 +81,17 @@
                 pl.BlockSpec((cols, width), lambda b, m: (0, 0)),
             ],
             out_specs=[
-                pl.BlockSpec((1, rows, width), lambda b, m: (b, 0, 0)),
+                pl.BlockSpec((parts, 1, sub, width), lambda b, m: (0, b, 0, 0)),
                 pl.BlockSpec((cols, width), lambda b, m: (0, 0)),
             ],
-        ),
-        compiler_params=pltpu.CompilerParams(vmem_limit_bytes=32 << 20),
+            scratch_shapes=[
+                pltpu.SMEM((tiles + 1,), jnp.int32),
+                pltpu.VMEM((width, cols), jnp.float32),
+            ],
+        ),
+        compiler_params=pltpu.CompilerParams(vmem_limit_bytes=52 << 20),
         cost_estimate=pl.CostEstimate(
-            flops=6 * blocks * rows * cols * width,
+            flops=24 * blocks * rows * cols * width,
             bytes_accessed=2 * blocks * rows * cols,
             transcendentals=0,
         ),
@@ -143,27 +168,34 @@
     thin = sub_rows // user_count
     total_blocks = blocks_here * user_count
 
-    dual_parts = dual.reshape(blocks_here, degree, user_count, thin, width).transpose(2, 0, 1, 3, 4)
-    dual_rows = lax.all_to_all(dual_parts, "user", 0, 0, tiled=True).reshape(
-        total_blocks, degree, thin, width
-    )
-
-    piece = lax.all_gather(user_factors, "item", axis=1, tiled=True)
-    user_term, item_term = gradients(tile_mask, piece, ratings, item_factors)
+    def exchange(parts, axis):
+        return lax.all_to_all(parts.astype(WIRE), axis, 0, 0, tiled=True).astype(jnp.float32)
+
     total_users = blocks_here * sub_rows * item_count * user_count
     total_items = item_cols * item_count
-    user_grad = lax.psum_scatter(user_term, "item", scatter_dimension=1, tiled=True) / math.sqrt(
-        total_items
-    )
-    item_grad = lax.psum(item_term, "user") / math.sqrt(total_users)
+    user_scale = 1.0 / math.sqrt(total_items)
+    item_scale = 1.0 / math.sqrt(total_users)
+
+    dual_parts = dual.reshape(blocks_here, degree, user_count, thin, width).transpose(2, 0, 1, 3, 4)
+    dual_rows = exchange(dual_parts, "user").reshape(total_blocks, degree, thin, width)
+
+    piece = lax.all_gather(user_factors, "item", axis=1, tiled=True)
+    user_term, item_term = gradients(tile_mask, piece, ratings, item_factors, item_count)
+    user_term, item_term, dual_rows = lax.optimization_barrier((user_term, item_term, dual_rows))
+
+    user_grad = jnp.sum(exchange(user_term * user_scale, "item"), axis=0)
+    item_parts = (item_term * item_scale).reshape(user_count, item_cols // user_count, width)
+    item_parts = exchange(item_parts, "user")
+    user_grad, item_parts = lax.optimization_barrier((user_grad, item_parts))
+    item_own = jnp.sum(item_parts, axis=0)
     target = user_factors.astype(jnp.float32) - descent * user_grad
     target_parts = target.reshape(blocks_here, user_count, thin, width).transpose(1, 0, 2, 3)
-    target_rows = lax.all_to_all(target_parts, "user", 0, 0, tiled=True).reshape(
-        total_blocks, thin, width
-    )
+    item_grad = lax.all_gather(item_own, "user", axis=0, tiled=True)
+    target_rows = exchange(target_parts, "user").reshape(total_blocks, thin, width)
     result = variation(neighbours, edge_weight, target_rows, dual_rows)
+    result, item_grad = lax.optimization_barrier((result, item_grad))
     result = result.reshape(user_count, blocks_here, degree + 1, thin, width)
-    result = lax.all_to_all(result, "user", 0, 0, tiled=True)
+    result = exchange(result, "user")
     result = result.transpose(1, 2, 0, 3, 4).reshape(blocks_here, degree + 1, sub_rows, width)
     return (result[:, degree], result[:, :degree], item_grad)
 

time: 294 us -> 187 us (0.64)
  waiting for transfers between devices: 199 us -> 92.5 us
  local copies, waits for them, and re-layouts: 18.1 us -> 5.88 us
  starting transfers between devices: 15.8 us -> 26.1 us
  other arithmetic: 4.18 us -> 10.1 us
  Pallas kernels: 41.5 us -> 36.9 us
    psum x1 -> x0, waiting for transfers between devices: 120 us -> none  [shards(): item_grad = lax.psum(item_term, 'user') / math.sqrt(total_users)]
    all_to_all x3 -> x5, waiting for transfers between devices: 32.9 us -> 69.1 us  [exchange(): lax.all_to_all(parts.astype(WIRE), axis, 0, 0, tiled=True)]
    reduce_scatter x1 -> x0, waiting for transfers between devices: 24.6 us -> none  [shards(): lax.psum_scatter(user_term, 'item', scatter_dimension=1, tiled=True)]
    all_gather x0 -> x1, waiting for transfers between devices: none -> 11.8 us  [shards(): item_grad = lax.all_gather(item_own, 'user', axis=0, tiled=True)]
    all_to_all x3 -> x5, starting transfers between devices: 15.7 us -> 26 us  [exchange(): lax.all_to_all(parts.astype(WIRE), axis, 0, 0, tiled=True)]
    all_gather x1, waiting for transfers between devices: 20.3 us -> 11 us  [shards(): piece = lax.all_gather(user_factors, 'item', axis=1, tiled=True)]
    unnamed x21 -> x20, local copies, waits for them, and re-layouts: 11.9 us -> 3.39 us
    convert_element_type x0 -> x6, other arithmetic: none -> 7.09 us  [the longest x5 7.02 us: exchange(): parts.astype(WIRE)]
  transfers between devices with their start and end apart: 6 -> 7, of which waited for: 5 -> 6; matrix products, arithmetic and copies ran while one was open for 2% -> 3% of each run, Pallas kernels for 0% -> 20%
where the time goes in v2:
time: 187 us; the launch traced here: 186 us
  waiting for transfers between devices  92.5 us (49%)
  Pallas kernels  36.9 us (20%)
  starting transfers between devices  26.1 us (14%)
  between operations  14.2 us (8%)
  other arithmetic  10.1 us (5%)
  local copies, waits for them, and re-layouts  5.88 us (3%)
    all_to_all x5, waiting for transfers between devices, exchange(): lax.all_to_all(parts.astype(WIRE), axis, 0, 0, tiled=True)  69.1 us
    pallas_call x1, Pallas kernels, gradients(): pl.pallas_call(functools.partial(gradient_kernel, tiles), out_shape=(jax....  26.8 us
    all_to_all x5, starting transfers between devices, exchange(): lax.all_to_all(parts.astype(WIRE), axis, 0, 0, tiled=True)  26 us
    all_gather x1, waiting for transfers between devices, shards(): item_grad = lax.all_gather(item_own, 'user', axis=0, tiled=True)  11.8 us
    all_gather x1, waiting for transfers between devices, shards(): piece = lax.all_gather(user_factors, 'item', axis=1, tiled=True)  11 us
    pallas_call x1, Pallas kernels, variation(): pl.pallas_call(functools.partial(variation_kernel, group), out_shape=jax....  10.1 us
    convert_element_type x5, other arithmetic, exchange(): parts.astype(WIRE)  7.02 us
  transfers between devices with their start and end apart: 7, of which 6 were waited for; matrix products, arithmetic and copies ran while one was open for 3% of the time, Pallas kernels for 20%

profile of v2, /device:TPU:0, one launch (start us, length us, event | category | flops | bytes accessed | tf_op | source)
XLA Modules:
  0.0 185.7 jit_solution(5877671199718446353)
XLA Ops:
  7.2 0.0 all-gather.3.cloned.1.call-start
  7.2 0.7 all-gather.3.cloned.1.call-update
  7.9 0.0 copy-start.5
  7.9 0.0 copy-start.1
  7.9 2.8 %copy_bitcast_fusion.1 = f16[8,16,4,8,128]{4,3,2,1,0:T(8,128)(2,1)} fusion(f32[16,4,64,128]{3,2,1,0:T(8,128)} %param.13), kind=kLoop, calls=%fused_computation.5 | loop fusion | flops 524288 | bytes 3145728 | tf_op jit(solution)/shard_map/convert_element_type | solution.py:172
  10.7 7.3 %all-to-all-start = ((f16[8,16,4,8,128]{4,3,2,1,0:T(8,128)(2,1)}), f16[8,16,4,8,128]{4,3,2,1,0:T(8,128)(2,1)S(1)}, u32[]{:S(2)}, u32[]{:S(2)}) async-start(f16[8,16,4,8,128]{4,3,2,1,0:T(8,128)(2,1)} %copy_bitcast_fusion.1), calls=%async_computation | async-start | bytes 2097152 | tf_op jit(solution)/shard_map/all_to_all | solution.py:172
  18.0 0.0 copy-done.5
  18.0 0.1 copy.16.mask_ref
  18.1 11.0 %all-gather.3.cloned.1.call-done.piece_ref = bf16[16,256,128]{2,1,0:T(8,128)(2,1)} async-done(((bf16[16,64,128]{2,1,0:T(8,128)(2,1)}), bf16[16,256,128]{2,1,0:T(8,128)(2,1)}) %all-gather.3.cloned.1.call-update) | async-done | bytes 1048592 | tf_op jit(solution)/shard_map/all_gather | solution.py:182
  29.0 0.0 copy-done.1
  29.0 26.8 %shard_map.94 = (f32[4,16,64,128]{3,2,1,0:T(8,128)}, f32[2048,128]{1,0:T(8,128)S(1)}) custom-call(s32[16,8]{1,0:T(8,128)S(1)} %copy.16.mask_ref, bf16[16,256,128]{2,1,0:T(8,128)(2,1)} %all-gather.3.cloned.1.call-done.piece_ref, bf16[4096,2048]{1,0:T(8,128)(2,1)} %rating_ref.1, bf16[2048,128]{1,0:T(8,128)(2,1)S(1)} %copy-done.1), custom_call_target="tpu_custom_call" | custom-call | flops 25769803776 | bytes 16777216 | tf_op jit(solution)/shard_map/pallas_call | solution.py:69
  55.8 0.0 all-to-all-done
  55.8 0.0 copy-start.2
  55.8 1.7 bitcast_convert_fusion.dual_ref
  57.5 0.5 copy-done.2
  58.0 1.3 multiply_convert_fusion
  59.3 3.5 %all-to-all-start.1 = ((f16[4,16,64,128]{3,2,1,0:T(8,128)(2,1)}), f16[4,16,64,128]{3,2,1,0:T(8,128)(2,1)S(1)}, u32[]{:S(2)}, u32[]{:S(2)}) async-start(f16[4,16,64,128]{3,2,1,0:T(8,128)(2,1)} %multiply_convert_fusion), calls=%async_computation.1 | async-start | bytes 2097152 | tf_op jit(solution)/shard_map/all_to_all | solution.py:172
  62.8 0.9 multiply_convert_fusion.1
  63.7 13.7 %all-to-all-done.1 = f16[4,16,64,128]{3,2,1,0:T(8,128)(2,1)S(1)} async-done(((f16[4,16,64,128]{3,2,1,0:T(8,128)(2,1)}), f16[4,16,64,128]{3,2,1,0:T(8,128)(2,1)S(1)}, u32[]{:S(2)}, u32[]{:S(2)}) %all-to-all-start.1) | async-done | bytes 1048608 | tf_op jit(solution)/shard_map/all_to_all | solution.py:172
  77.4 8.0 %all-to-all-start.2 = ((f16[8,256,128]{2,1,0:T(8,128)(2,1)}), f16[8,256,128]{2,1,0:T(8,128)(2,1)S(1)}, u32[]{:S(2)}, u32[]{:S(2)}) async-start(f16[8,256,128]{2,1,0:T(8,128)(2,1)} %bitcast.3), calls=%async_computation.2 | async-start | bytes 1048576 | tf_op jit(solution)/shard_map/all_to_all | solution.py:172
  85.5 0.0 copy-start.4
  85.5 0.0 all-gather.5.cloned.1.call-start
  85.5 0.2 convert_reduce_fusion
  85.8 0.0 copy-start.6
  85.8 0.0 copy-start.7
  85.8 14.0 %all-to-all-done.2 = f16[8,256,128]{2,1,0:T(8,128)(2,1)S(1)} async-done(((f16[8,256,128]{2,1,0:T(8,128)(2,1)}), f16[8,256,128]{2,1,0:T(8,128)(2,1)S(1)}, u32[]{:S(2)}, u32[]{:S(2)}) %all-to-all-start.2) | async-done | bytes 524320 | tf_op jit(solution)/shard_map/all_to_all | solution.py:172
  99.8 0.1 convert_element_type.53
  99.8 0.7 reduce_sum.19
  100.6 0.0 all-gather.5.cloned.1.call-update
  100.6 0.0 copy-done.4
  100.6 0.8 copy_bitcast_fusion.2
  101.4 3.6 %all-to-all-start.3 = ((f16[8,16,8,128]{3,2,1,0:T(8,128)(2,1)}), f16[8,16,8,128]{3,2,1,0:T(8,128)(2,1)S(1)}, u32[]{:S(2)}, u32[]{:S(2)}) async-start(f16[8,16,8,128]{3,2,1,0:T(8,128)(2,1)} %copy_bitcast_fusion.2), calls=%async_computation.3 | async-start | bytes 524288 | tf_op jit(solution)/shard_map/all_to_all | solution.py:172
  105.0 0.0 copy-done.6
  105.0 0.1 copy.14
  105.1 0.1 reshape.37.near_ref
  105.2 0.0 copy-done.7
  105.2 0.1 copy.15
  105.4 0.1 reshape.38.weight_ref
  105.5 11.3 %all-to-all-done.3 = f16[8,16,8,128]{3,2,1,0:T(8,128)(2,1)S(1)} async-done(((f16[8,16,8,128]{3,2,1,0:T(8,128)(2,1)}), f16[8,16,8,128]{3,2,1,0:T(8,128)(2,1)S(1)}, u32[]{:S(2)}, u32[]{:S(2)}) %all-to-all-start.3) | async-done | bytes 262176 | tf_op jit(solution)/shard_map/all_to_all | solution.py:172
  116.8 0.1 bitcast_convert_fusion.1.target_ref
  116.8 0.0 copy-start
  116.8 1.6 copy-done
  118.4 10.1 %shard_map.95 = f32[128,5,8,128]{3,2,1,0:T(8,128)S(1)} custom-call(s32[512]{0:T(512)S(1)} %reshape.37.near_ref, f32[512]{0:T(512)S(1)} %reshape.38.weight_ref, f32[128,8,128]{2,1,0:T(8,128)S(1)} %bitcast_convert_fusion.1.target_ref, f32[128,4,8,128]{3,2,1,0:T(8,128)S(1)} %copy-done), custom_call_target="tpu_custom_call" | custom-call | flops 20971520 | bytes 4194304 | tf_op jit(solution)/shard_map/pallas_call | solution.py:146
  128.6 11.8 %all-gather.5.cloned.1.call-done = f32[2048,128]{1,0:T(8,128)} async-done(((f32[256,128]{1,0:T(8,128)}), f32[2048,128]{1,0:T(8,128)}) %all-gather.5.cloned.1.call-update) | async-done | bytes 1048592 | tf_op jit(solution)/shard_map/all_gather | solution.py:193
  140.3 1.2 convert_element_type.57
  141.5 3.6 %all-to-all-start.4 = ((f16[8,16,5,8,128]{4,3,2,1,0:T(8,128)(2,1)}), f16[8,16,5,8,128]{4,3,2,1,0:T(8,128)(2,1)S(1)}, u32[]{:S(2)}, u32[]{:S(2)}) async-start(f16[8,16,5,8,128]{4,3,2,1,0:T(8,128)(2,1)} %bitcast.25), calls=%async_computation.4 | async-start | bytes 2621440 | tf_op jit(solution)/shard_map/all_to_all | solution.py:172
  145.1 30.1 %all-to-all-done.4 = f16[8,16,5,8,128]{4,3,2,1,0:T(8,128)(2,1)S(1)} async-done(((f16[8,16,5,8,128]{4,3,2,1,0:T(8,128)(2,1)}), f16[8,16,5,8,128]{4,3,2,1,0:T(8,128)(2,1)S(1)}, u32[]{:S(2)}, u32[]{:S(2)}) %all-to-all-start.4) | async-done | bytes 1310752 | tf_op jit(solution)/shard_map/all_to_all | solution.py:172
  175.2 0.3 copy_bitcast_fusion
  175.6 0.0 copy-start.3
  175.6 1.5 slice.9
  177.0 0.8 slice_bitcast_fusion
  177.9 0.0 copy-done.3
  177.9 1.0 copy.24
Async XLA Ops:
  7.2 21.9 %all-gather.3.cloned.1.call-start = ((), (), s32[]{:S(2)}) async-start(), calls=%async_computation.5 | async-start | bytes 1310720 | tf_op jit(solution)/shard_map/all_gather | solution.py:182
  7.9 10.1 %copy-start.5 = (s32[16,8]{0,1:T(8,128)S(1)}, s32[16,8]{0,1:T(8,128)}, u32[]{:S(2)}) copy-start(s32[16,8]{0,1:T(8,128)} %param.8) | copy-start | bytes 1540
  7.9 21.1 %copy-start.1 = (bf16[2048,128]{1,0:T(8,128)(2,1)S(1)}, bf16[2048,128]{1,0:T(8,128)(2,1)}, u32[]{:S(2)}) copy-start(bf16[2048,128]{1,0:T(8,128)(2,1)} %item_ref.1) | copy-start | bytes 1572868
  10.7 45.1 %all-to-all-start = ((f16[8,16,4,8,128]{4,3,2,1,0:T(8,128)(2,1)}), f16[8,16,4,8,128]{4,3,2,1,0:T(8,128)(2,1)S(1)}, u32[]{:S(2)}, u32[]{:S(2)}) async-start(f16[8,16,4,8,128]{4,3,2,1,0:T(8,128)(2,1)} %copy_bitcast_fusion.1), calls=%async_computation | async-start | bytes 2097152 | tf_op jit(solution)/shard_map/all_to_all | solution.py:172
  55.8 2.2 %copy-start.2 = (f32[4,16,64,128]{3,2,1,0:T(8,128)S(1)}, f32[4,16,64,128]{3,2,1,0:T(8,128)}, u32[]{:S(2)}) copy-start(f32[4,16,64,128]{3,2,1,0:T(8,128)} %get-tuple-element.14) | copy-start | bytes 6291460
  59.3 18.1 %all-to-all-start.1 = ((f16[4,16,64,128]{3,2,1,0:T(8,128)(2,1)}), f16[4,16,64,128]{3,2,1,0:T(8,128)(2,1)S(1)}, u32[]{:S(2)}, u32[]{:S(2)}) async-start(f16[4,16,64,128]{3,2,1,0:T(8,128)(2,1)} %multiply_convert_fusion), calls=%async_computation.1 | async-start | bytes 2097152 | tf_op jit(solution)/shard_map/all_to_all | solution.py:172
  77.4 22.3 %all-to-all-start.2 = ((f16[8,256,128]{2,1,0:T(8,128)(2,1)}), f16[8,256,128]{2,1,0:T(8,128)(2,1)S(1)}, u32[]{:S(2)}, u32[]{:S(2)}) async-start(f16[8,256,128]{2,1,0:T(8,128)(2,1)} %bitcast.3), calls=%async_computation.2 | async-start | bytes 1048576 | tf_op jit(solution)/shard_map/all_to_all | solution.py:172
  85.5 15.1 %copy-start.4 = (bf16[16,64,128]{2,1,0:T(8,128)(2,1)S(1)}, bf16[16,64,128]{2,1,0:T(8,128)(2,1)}, u32[]{:S(2)}) copy-start(bf16[16,64,128]{2,1,0:T(8,128)(2,1)} %param.9) | copy-start | bytes 786436
  85.5 54.9 %all-gather.5.cloned.1.call-start = ((), (), s32[]{:S(2)}) async-start(), calls=%async_computation.6 | async-start | bytes 1179648 | tf_op jit(solution)/shard_map/all_gather | solution.py:193
  85.8 19.2 %copy-start.6 = (s32[128,4]{0,1:T(4,128)S(1)}, s32[128,4]{0,1:T(4,128)}, u32[]{:S(2)}) copy-start(s32[128,4]{0,1:T(4,128)} %param.11) | copy-start | bytes 6148
  85.8 19.5 %copy-start.7 = (f32[128,4]{0,1:T(4,128)S(1)}, f32[128,4]{0,1:T(4,128)}, u32[]{:S(2)}) copy-start(f32[128,4]{0,1:T(4,128)} %param.12) | copy-start | bytes 6148
  101.4 15.4 %all-to-all-start.3 = ((f16[8,16,8,128]{3,2,1,0:T(8,128)(2,1)}), f16[8,16,8,128]{3,2,1,0:T(8,128)(2,1)S(1)}, u32[]{:S(2)}, u32[]{:S(2)}) async-start(f16[8,16,8,128]{3,2,1,0:T(8,128)(2,1)} %copy_bitcast_fusion.2), calls=%async_computation.3 | async-start | bytes 524288 | tf_op jit(solution)/shard_map/all_to_all | solution.py:172
  116.8 1.6 copy-start
  141.5 33.7 %all-to-all-start.4 = ((f16[8,16,5,8,128]{4,3,2,1,0:T(8,128)(2,1)}), f16[8,16,5,8,128]{4,3,2,1,0:T(8,128)(2,1)S(1)}, u32[]{:S(2)}, u32[]{:S(2)}) async-start(f16[8,16,5,8,128]{4,3,2,1,0:T(8,128)(2,1)} %bitcast.25), calls=%async_computation.4 | async-start | bytes 2621440 | tf_op jit(solution)/shard_map/all_to_all | solution.py:172
  175.6 2.3 %copy-start.3 = (f32[2048,128]{1,0:T(8,128)S(1)}, f32[2048,128]{1,0:T(8,128)}, u32[]{:S(2)}) copy-start(f32[2048,128]{1,0:T(8,128)} %all-gather.5.cloned.1.call-done) | copy-start | bytes 3145732
Sparse Core Ops, SparseCore 0:
  9.6 19.4 all-gather.2
  100.7 39.5 all-gather.4

commit v3 on v2

--- a/solution.py
+++ b/solution.py
@@ -9,7 +9,6 @@
 from jax.sharding import PartitionSpec as P
 
 ITERS = 2
-PAIR = 2
 WIRE = jnp.float16
 
 descent = 0.5
@@ -17,44 +16,24 @@
 primal_step = 0.25
 
 
-def gradient_kernel(tiles, mask_ref, piece_ref, rating_ref, item_ref, user_out, item_out, active, total):
+def gradient_kernel(seen_ref, piece_ref, rating_ref, item_ref, user_out, item_out, total):
     b = pl.program_id(0)
-    width = item_ref.shape[0] // tiles
-    parts, _, sub, rank = user_out.shape
+    parts, _, sub, _ = user_out.shape
 
     @pl.when(b == 0)
     def _():
         total[...] = jnp.zeros_like(total)
 
-    count = 0
-    for t in range(tiles):
-        active[count] = t
-        count = count + jnp.where(mask_ref[b, t] != 0, 1, 0)
-
-    user_out[...] = jnp.zeros_like(user_out)
     users = piece_ref[0]
-    across = users.T
-
-    def pair(step, _):
-        first = step * PAIR
-        user_sum = None
-        for j in range(PAIR):
-            at = jnp.minimum(first + j, count - 1)
-            keep = jnp.where(first + j < count, 1.0, 0.0)
-            cols = pl.ds(pl.multiple_of(active[at] * width, width), width)
-            items = item_ref[cols, :]
-            scores = lax.dot_general(
-                users, items, (((1,), (1,)), ((), ())), preferred_element_type=jnp.float32
-            )
-            errors = (keep * (scores - rating_ref[:, cols].astype(jnp.float32))).astype(jnp.bfloat16)
-            term = jnp.dot(errors, items, preferred_element_type=jnp.float32)
-            user_sum = term if user_sum is None else user_sum + term
-            total[:, cols] += jnp.dot(across, errors, preferred_element_type=jnp.float32)
-        for p in range(parts):
-            user_out[p, 0] += user_sum[p * sub : (p + 1) * sub]
-        return 0
-
-    lax.fori_loop(0, (count + PAIR - 1) // PAIR, pair, 0)
+    items = item_ref[...]
+    scores = lax.dot_general(
+        users, items, (((1,), (1,)), ((), ())), preferred_element_type=jnp.float32
+    )
+    errors = (seen_ref[0] * (scores - rating_ref[...].astype(jnp.float32))).astype(jnp.bfloat16)
+    term = jnp.dot(errors, items, preferred_element_type=jnp.float32)
+    for p in range(parts):
+        user_out[p, 0] = term[p * sub : (p + 1) * sub]
+    total[...] += jnp.dot(users.T, errors, preferred_element_type=jnp.float32)
 
     @pl.when(b == pl.num_programs(0) - 1)
     def _():
@@ -64,38 +43,33 @@
 def gradients(tile_mask, piece, ratings, item_factors, parts):
     blocks, rows, width = piece.shape
     cols = item_factors.shape[0]
-    tiles = tile_mask.shape[1]
     sub = rows // parts
+    seen = jnp.repeat(tile_mask.astype(jnp.float32), cols // tile_mask.shape[1], axis=1)
     return pl.pallas_call(
-        functools.partial(gradient_kernel, tiles),
+        gradient_kernel,
         out_shape=(
             jax.ShapeDtypeStruct((parts, blocks, sub, width), jnp.float32),
             jax.ShapeDtypeStruct((cols, width), jnp.float32),
         ),
-        grid_spec=pltpu.PrefetchScalarGridSpec(
-            num_scalar_prefetch=1,
-            grid=(blocks,),
-            in_specs=[
-                pl.BlockSpec((1, rows, width), lambda b, m: (b, 0, 0)),
-                pl.BlockSpec((rows, cols), lambda b, m: (b, 0)),
-                pl.BlockSpec((cols, width), lambda b, m: (0, 0)),
-            ],
-            out_specs=[
-                pl.BlockSpec((parts, 1, sub, width), lambda b, m: (0, b, 0, 0)),
-                pl.BlockSpec((cols, width), lambda b, m: (0, 0)),
-            ],
-            scratch_shapes=[
-                pltpu.SMEM((tiles + 1,), jnp.int32),
-                pltpu.VMEM((width, cols), jnp.float32),
-            ],
-        ),
+        grid=(blocks,),
+        in_specs=[
+            pl.BlockSpec((1, 1, cols), lambda b: (b, 0, 0)),
+            pl.BlockSpec((1, rows, width), lambda b: (b, 0, 0)),
+            pl.BlockSpec((rows, cols), lambda b: (b, 0)),
+            pl.BlockSpec((cols, width), lambda b: (0, 0)),
+        ],
+        out_specs=[
+            pl.BlockSpec((parts, 1, sub, width), lambda b: (0, b, 0, 0)),
+            pl.BlockSpec((cols, width), lambda b: (0, 0)),
+        ],
+        scratch_shapes=[pltpu.VMEM((width, cols), jnp.float32)],
         compiler_params=pltpu.CompilerParams(vmem_limit_bytes=52 << 20),
         cost_estimate=pl.CostEstimate(
             flops=24 * blocks * rows * cols * width,
             bytes_accessed=2 * blocks * rows * cols,
             transcendentals=0,
         ),
-    )(tile_mask, piece, ratings, item_factors)
+    )(seen[:, None, :], piece, ratings, item_factors)
 
 
 def variation_kernel(group, near_ref, weight_ref, target_ref, dual_ref, out_ref, extra_ref, div_ref):
@@ -184,16 +158,16 @@
     user_term, item_term, dual_rows = lax.optimization_barrier((user_term, item_term, dual_rows))
 
     user_grad = jnp.sum(exchange(user_term * user_scale, "item"), axis=0)
-    item_parts = (item_term * item_scale).reshape(user_count, item_cols // user_count, width)
-    item_parts = exchange(item_parts, "user")
-    user_grad, item_parts = lax.optimization_barrier((user_grad, item_parts))
-    item_own = jnp.sum(item_parts, axis=0)
+    item_own = lax.psum_scatter(item_term, "user", scatter_dimension=0, tiled=True)
+    user_grad, item_own = lax.optimization_barrier((user_grad, item_own))
+    item_own = (item_own * (item_scale / user_count)).astype(WIRE)
     target = user_factors.astype(jnp.float32) - descent * user_grad
     target_parts = target.reshape(blocks_here, user_count, thin, width).transpose(1, 0, 2, 3)
     item_grad = lax.all_gather(item_own, "user", axis=0, tiled=True)
     target_rows = exchange(target_parts, "user").reshape(total_blocks, thin, width)
     result = variation(neighbours, edge_weight, target_rows, dual_rows)
     result, item_grad = lax.optimization_barrier((result, item_grad))
+    item_grad = item_grad.astype(jnp.float32) * user_count
     result = result.reshape(user_count, blocks_here, degree + 1, thin, width)
     result = exchange(result, "user")
     result = result.transpose(1, 2, 0, 3, 4).reshape(blocks_here, degree + 1, sub_rows, width)

time: 187 us -> 202 us (1.080)
  blocking collectives: 0 us -> 49.2 us
  waiting for transfers between devices: 92.5 us -> 78.3 us
  starting transfers between devices: 26.1 us -> 16.3 us
  Pallas kernels: 36.9 us -> 30.1 us
  local copies, waits for them, and re-layouts: 5.88 us -> 3.03 us
    all_to_all x5 -> x3, waiting for transfers between devices: 69.1 us -> 22.7 us  [exchange(): lax.all_to_all(parts.astype(WIRE), axis, 0, 0, tiled=True)]
    reduce_scatter x0 -> x1, waiting for transfers between devices: none -> 44.3 us  [shards(): lax.psum_scatter(item_term, 'user', scatter_dimension=0, tiled=True)]
    all_gather x0 -> x1, blocking collectives: none -> 32.2 us  [shards(): item_grad = lax.all_gather(item_own, 'user', axis=0, tiled=True)]
    all_to_all x0 -> x1, blocking collectives: none -> 17 us  [exchange(): lax.all_to_all(parts.astype(WIRE), axis, 0, 0, tiled=True)]
    all_gather x1 -> x0, waiting for transfers between devices: 11.8 us -> none  [shards(): item_grad = lax.all_gather(item_own, 'user', axis=0, tiled=True)]
    all_to_all x5 -> x3, starting transfers between devices: 26 us -> 16.2 us  [exchange(): lax.all_to_all(parts.astype(WIRE), axis, 0, 0, tiled=True)]
    pallas_call x1, Pallas kernels: 26.8 us -> 20 us  [gradients(): pl.pallas_call(gradient_kernel, out_shape=(jax.ShapeDtypeStruct((parts, b...]
    unnamed x20 -> x12, local copies, waits for them, and re-layouts: 3.39 us -> 0.25 us
  transfers between devices with their start and end apart: 7 -> 5, of which waited for: 6 -> 3; matrix products, arithmetic and copies ran while one was open for 3% -> 4% of each run, Pallas kernels for 20% -> 10%
where the time goes in v3:
time: 202 us; the launch traced here: 201 us
  waiting for transfers between devices  78.3 us (39%)
  blocking collectives  49.2 us (24%)
  Pallas kernels  30.1 us (15%)
  starting transfers between devices  16.3 us (8%)
  between operations  14.2 us (7%)
  other arithmetic  9.74 us (5%)
  local copies, waits for them, and re-layouts  3.03 us (2%)
    reduce_scatter x1, waiting for transfers between devices, shards(): lax.psum_scatter(item_term, 'user', scatter_dimension=0, tiled=True)  44.3 us
    all_gather x1, blocking collectives, shards(): item_grad = lax.all_gather(item_own, 'user', axis=0, tiled=True)  32.2 us
    all_to_all x3, waiting for transfers between devices, exchange(): lax.all_to_all(parts.astype(WIRE), axis, 0, 0, tiled=True)  22.7 us
    pallas_call x1, Pallas kernels, gradients(): pl.pallas_call(gradient_kernel, out_shape=(jax.ShapeDtypeStruct((parts, b...  20 us
    all_to_all x1, blocking collectives, exchange(): lax.all_to_all(parts.astype(WIRE), axis, 0, 0, tiled=True)  17 us
    all_to_all x3, starting transfers between devices, exchange(): lax.all_to_all(parts.astype(WIRE), axis, 0, 0, tiled=True)  16.2 us
    all_gather x1, waiting for transfers between devices, shards(): piece = lax.all_gather(user_factors, 'item', axis=1, tiled=True)  10.6 us
    pallas_call x1, Pallas kernels, variation(): pl.pallas_call(functools.partial(variation_kernel, group), out_shape=jax....  10.1 us
  transfers between devices with their start and end apart: 5, of which 3 were waited for; matrix products, arithmetic and copies ran while one was open for 4% of the time, Pallas kernels for 10%

profile of v3, /device:TPU:0, one launch (start us, length us, event | category | flops | bytes accessed | tf_op | source)
XLA Modules:
  0.0 200.9 jit_solution(4983038222587260137)
XLA Ops:
  7.2 0.0 all-gather.2.cloned.1.call-start
  7.2 0.7 all-gather.2.cloned.1.call-update
  7.9 0.0 copy-start.2
  7.9 0.0 copy-start
  7.9 2.8 %copy_bitcast_fusion.1 = f16[8,16,4,8,128]{4,3,2,1,0:T(8,128)(2,1)} fusion(f32[16,4,64,128]{3,2,1,0:T(8,128)} %param.13), kind=kLoop, calls=%fused_computation.5 | loop fusion | flops 524288 | bytes 3145728 | tf_op jit(solution)/shard_map/convert_element_type | solution.py:146
  10.8 7.3 %all-to-all-start = ((f16[8,16,4,8,128]{4,3,2,1,0:T(8,128)(2,1)}), f16[8,16,4,8,128]{4,3,2,1,0:T(8,128)(2,1)S(1)}, u32[]{:S(2)}, u32[]{:S(2)}) async-start(f16[8,16,4,8,128]{4,3,2,1,0:T(8,128)(2,1)} %copy_bitcast_fusion.1), calls=%async_computation | async-start | bytes 2097152 | tf_op jit(solution)/shard_map/all_to_all | solution.py:146
  18.0 0.0 reduce-scatter.2.cloned.1.call-start
  18.1 0.0 copy-done.2
  18.1 0.1 copy.16
  18.2 0.1 broadcast_in_dim.3
  18.2 0.1 broadcast_in_dim_reshape.3.seen_ref
  18.4 10.6 %all-gather.2.cloned.1.call-done.piece_ref = bf16[16,256,128]{2,1,0:T(8,128)(2,1)} async-done(((bf16[16,64,128]{2,1,0:T(8,128)(2,1)}), bf16[16,256,128]{2,1,0:T(8,128)(2,1)}) %all-gather.2.cloned.1.call-update) | async-done | bytes 1048592 | tf_op jit(solution)/shard_map/all_gather | solution.py:156
  29.0 0.0 copy-done
  29.0 20.0 %shard_map.94 = (f32[4,16,64,128]{3,2,1,0:T(8,128)}, f32[2048,128]{1,0:T(8,128)}) custom-call(f32[16,1,2048]{2,1,0:T(1,128)S(1)} %broadcast_in_dim_reshape.3.seen_ref, bf16[16,256,128]{2,1,0:T(8,128)(2,1)} %all-gather.2.cloned.1.call-done.piece_ref, bf16[4096,2048]{1,0:T(8,128)(2,1)} %rating_ref.1, bf16[2048,128]{1,0:T(8,128)(2,1)S(1)} %copy-done), custom_call_target="tpu_custom_call" | custom-call | flops 25769803776 | bytes 16777216 | tf_op jit(solution)/shard_map/pallas_call | solution.py:48
  49.0 0.0 all-to-all-done
  49.0 0.3 bitcast_convert_fusion.dual_ref
  49.4 0.0 reduce-scatter.2.cloned.1.call-update
  49.4 1.9 multiply_convert_fusion
  51.4 0.0 copy-start.1
  51.4 0.0 copy-start.3
  51.4 17.0 %all_to_all.20 = f16[4,16,64,128]{3,2,1,0:T(8,128)(2,1)S(1)} all-to-all(f16[4,16,64,128]{3,2,1,0:T(8,128)(2,1)S(1)} %multiply_convert_fusion), channel_id=1, replica_groups=mesh['user'=8,'item'=4] {'item'}, dimensions={0} | all-to-all | bytes 2097152 | tf_op jit(solution)/shard_map/all_to_all | solution.py:146
  68.4 0.0 copy-start.4
  68.4 0.2 convert_reduce_fusion
  68.6 44.3 %reduce-scatter.2.cloned.1.call-done = f32[256,128]{1,0:T(8,128)} async-done(((f32[2048,128]{1,0:T(8,128)}), f32[256,128]{1,0:T(8,128)}) %reduce-scatter.2.cloned.1.call-update) | async-done | bytes 131088 | tf_op jit(solution)/shard_map/reduce_scatter | solution.py:161
  112.9 0.0 copy-done.1
  112.9 0.8 copy_bitcast_fusion.2
  113.7 3.6 %all-to-all-start.2 = ((f16[8,16,8,128]{3,2,1,0:T(8,128)(2,1)}), f16[8,16,8,128]{3,2,1,0:T(8,128)(2,1)S(1)}, u32[]{:S(2)}, u32[]{:S(2)}) async-start(f16[8,16,8,128]{3,2,1,0:T(8,128)(2,1)} %copy_bitcast_fusion.2), calls=%async_computation.3 | async-start | bytes 524288 | tf_op jit(solution)/shard_map/all_to_all | solution.py:146
  117.3 0.0 copy-done.3
  117.3 0.1 copy.14
  117.4 0.1 reshape.35.near_ref
  117.5 0.0 copy-done.4
  117.5 0.1 copy.15
  117.6 0.1 reshape.36.weight_ref
  117.8 0.9 multiply_convert_fusion.1
  118.7 32.2 %all_gather.7 = f16[2048,128]{1,0:T(8,128)(2,1)S(1)} all-gather(f16[256,128]{1,0:T(8,128)(2,1)S(1)} %multiply_convert_fusion.1), channel_id=1, replica_groups=mesh['user'=8,'item'=4] {'user'}, dimensions={0}, use_global_device_ids=true | all-gather | bytes 589824 | tf_op jit(solution)/shard_map/all_gather | solution.py:166
  150.9 0.0 all-to-all-done.2
  150.9 0.1 bitcast_convert_fusion.1.target_ref
  151.0 10.1 %shard_map.95 = f32[128,5,8,128]{3,2,1,0:T(8,128)S(1)} custom-call(s32[512]{0:T(512)S(1)} %reshape.35.near_ref, f32[512]{0:T(512)S(1)} %reshape.36.weight_ref, f32[128,8,128]{2,1,0:T(8,128)S(1)} %bitcast_convert_fusion.1.target_ref, f32[128,4,8,128]{3,2,1,0:T(8,128)S(1)} %bitcast_convert_fusion.dual_ref), custom_call_target="tpu_custom_call" | custom-call | flops 20971520 | bytes 4194304 | tf_op jit(solution)/shard_map/pallas_call | solution.py:120
  161.1 1.2 convert_element_type.56
  162.3 5.4 %all-to-all-start.3 = ((f16[8,16,5,8,128]{4,3,2,1,0:T(8,128)(2,1)}), f16[8,16,5,8,128]{4,3,2,1,0:T(8,128)(2,1)S(1)}, u32[]{:S(2)}, u32[]{:S(2)}) async-start(f16[8,16,5,8,128]{4,3,2,1,0:T(8,128)(2,1)} %bitcast.6), calls=%async_computation.4 | async-start | bytes 2621440 | tf_op jit(solution)/shard_map/all_to_all | solution.py:146
  167.7 1.1 convert_multiply_fusion
  168.7 22.7 %all-to-all-done.3 = f16[8,16,5,8,128]{4,3,2,1,0:T(8,128)(2,1)S(1)} async-done(((f16[8,16,5,8,128]{4,3,2,1,0:T(8,128)(2,1)}), f16[8,16,5,8,128]{4,3,2,1,0:T(8,128)(2,1)S(1)}, u32[]{:S(2)}, u32[]{:S(2)}) %all-to-all-start.3) | async-done | bytes 1310752 | tf_op jit(solution)/shard_map/all_to_all | solution.py:146
  191.4 0.3 copy_bitcast_fusion
  191.7 1.5 slice.9
  193.2 0.8 slice_bitcast_fusion
  (1 shorter events, 0.0 us)
Async XLA Ops:
  7.2 21.9 %all-gather.2.cloned.1.call-start = ((), (), s32[]{:S(2)}) async-start(), calls=%async_computation.5 | async-start | bytes 1310720 | tf_op jit(solution)/shard_map/all_gather | solution.py:156
  7.9 10.2 %copy-start.2 = (s32[16,8]{0,1:T(8,128)S(1)}, s32[16,8]{0,1:T(8,128)}, u32[]{:S(2)}) copy-start(s32[16,8]{0,1:T(8,128)} %param.8) | copy-start | bytes 1540
  7.9 21.1 %copy-start = (bf16[2048,128]{1,0:T(8,128)(2,1)S(1)}, bf16[2048,128]{1,0:T(8,128)(2,1)}, u32[]{:S(2)}) copy-start(bf16[2048,128]{1,0:T(8,128)(2,1)} %item_ref.1) | copy-start | bytes 1572868
  10.8 38.3 %all-to-all-start = ((f16[8,16,4,8,128]{4,3,2,1,0:T(8,128)(2,1)}), f16[8,16,4,8,128]{4,3,2,1,0:T(8,128)(2,1)S(1)}, u32[]{:S(2)}, u32[]{:S(2)}) async-start(f16[8,16,4,8,128]{4,3,2,1,0:T(8,128)(2,1)} %copy_bitcast_fusion.1), calls=%async_computation | async-start | bytes 2097152 | tf_op jit(solution)/shard_map/all_to_all | solution.py:146
  18.0 94.9 %reduce-scatter.2.cloned.1.call-start = ((), (), s32[]{:S(2)}) async-start(), calls=%async_computation.6 | async-start | bytes 1179648 | tf_op jit(solution)/shard_map/reduce_scatter | solution.py:161
  51.4 61.5 %copy-start.1 = (bf16[16,64,128]{2,1,0:T(8,128)(2,1)S(1)}, bf16[16,64,128]{2,1,0:T(8,128)(2,1)}, u32[]{:S(2)}) copy-start(bf16[16,64,128]{2,1,0:T(8,128)(2,1)} %param.9) | copy-start | bytes 786436
  51.4 65.9 %copy-start.3 = (s32[128,4]{0,1:T(4,128)S(1)}, s32[128,4]{0,1:T(4,128)}, u32[]{:S(2)}) copy-start(s32[128,4]{0,1:T(4,128)} %param.11) | copy-start | bytes 6148
  68.4 49.1 %copy-start.4 = (f32[128,4]{0,1:T(4,128)S(1)}, f32[128,4]{0,1:T(4,128)}, u32[]{:S(2)}) copy-start(f32[128,4]{0,1:T(4,128)} %param.12) | copy-start | bytes 6148
  113.7 37.2 %all-to-all-start.2 = ((f16[8,16,8,128]{3,2,1,0:T(8,128)(2,1)}), f16[8,16,8,128]{3,2,1,0:T(8,128)(2,1)S(1)}, u32[]{:S(2)}, u32[]{:S(2)}) async-start(f16[8,16,8,128]{3,2,1,0:T(8,128)(2,1)} %copy_bitcast_fusion.2), calls=%async_computation.3 | async-start | bytes 524288 | tf_op jit(solution)/shard_map/all_to_all | solution.py:146
  162.3 29.1 %all-to-all-start.3 = ((f16[8,16,5,8,128]{4,3,2,1,0:T(8,128)(2,1)}), f16[8,16,5,8,128]{4,3,2,1,0:T(8,128)(2,1)S(1)}, u32[]{:S(2)}, u32[]{:S(2)}) async-start(f16[8,16,5,8,128]{4,3,2,1,0:T(8,128)(2,1)} %bitcast.6), calls=%async_computation.4 | async-start | bytes 2621440 | tf_op jit(solution)/shard_map/all_to_all | solution.py:146
Sparse Core Ops, SparseCore 0:
  9.6 19.4 all-gather.1
  49.5 63.3 reduce-scatter.1

commit v4 on v3

--- a/solution.py
+++ b/solution.py
@@ -158,16 +158,16 @@
     user_term, item_term, dual_rows = lax.optimization_barrier((user_term, item_term, dual_rows))
 
     user_grad = jnp.sum(exchange(user_term * user_scale, "item"), axis=0)
-    item_own = lax.psum_scatter(item_term, "user", scatter_dimension=0, tiled=True)
-    user_grad, item_own = lax.optimization_barrier((user_grad, item_own))
-    item_own = (item_own * (item_scale / user_count)).astype(WIRE)
+    item_parts = (item_term * item_scale).reshape(user_count, item_cols // user_count, width)
+    item_parts = exchange(item_parts, "user")
+    user_grad, item_parts = lax.optimization_barrier((user_grad, item_parts))
+    item_own = jnp.sum(item_parts, axis=0)
     target = user_factors.astype(jnp.float32) - descent * user_grad
     target_parts = target.reshape(blocks_here, user_count, thin, width).transpose(1, 0, 2, 3)
     item_grad = lax.all_gather(item_own, "user", axis=0, tiled=True)
     target_rows = exchange(target_parts, "user").reshape(total_blocks, thin, width)
     result = variation(neighbours, edge_weight, target_rows, dual_rows)
     result, item_grad = lax.optimization_barrier((result, item_grad))
-    item_grad = item_grad.astype(jnp.float32) * user_count
     result = result.reshape(user_count, blocks_here, degree + 1, thin, width)
     result = exchange(result, "user")
     result = result.transpose(1, 2, 0, 3, 4).reshape(blocks_here, degree + 1, sub_rows, width)

time: 202 us -> 177 us (0.88)
  blocking collectives: 49.2 us -> 0 us
  waiting for transfers between devices: 78.3 us -> 92.7 us
  starting transfers between devices: 16.3 us -> 23.5 us
  local copies, waits for them, and re-layouts: 3.03 us -> 6.09 us
    all_to_all x3 -> x5, waiting for transfers between devices: 22.7 us -> 69.6 us  [exchange(): lax.all_to_all(parts.astype(WIRE), axis, 0, 0, tiled=True)]
    reduce_scatter x1 -> x0, waiting for transfers between devices: 44.3 us -> none  [shards(): lax.psum_scatter(item_term, 'user', scatter_dimension=0, tiled=True)]
    all_gather x1 -> x0, blocking collectives: 32.2 us -> none  [shards(): item_grad = lax.all_gather(item_own, 'user', axis=0, tiled=True)]
    all_to_all x1 -> x0, blocking collectives: 17 us -> none  [exchange(): lax.all_to_all(parts.astype(WIRE), axis, 0, 0, tiled=True)]
    all_gather x0 -> x1, waiting for transfers between devices: none -> 11.7 us  [shards(): item_grad = lax.all_gather(item_own, 'user', axis=0, tiled=True)]
    all_to_all x3 -> x5, starting transfers between devices: 16.2 us -> 23.5 us  [exchange(): lax.all_to_all(parts.astype(WIRE), axis, 0, 0, tiled=True)]
    unnamed x12 -> x19, local copies, waits for them, and re-layouts: 0.25 us -> 3.32 us
    convert_element_type x4 -> x5, other arithmetic: 6.78 us -> 7.02 us  [exchange(): parts.astype(WIRE)]
  transfers between devices with their start and end apart: 5 -> 7, of which waited for: 3 -> 6; matrix products, arithmetic and copies ran while one was open for 4% -> 3% of each run, Pallas kernels for 10% -> 17%
where the time goes in v4:
time: 177 us; the launch traced here: 176 us
  waiting for transfers between devices  92.7 us (52%)
  Pallas kernels  29.8 us (17%)
  starting transfers between devices  23.5 us (13%)
  between operations  14.2 us (8%)
  other arithmetic  10.1 us (6%)
  local copies, waits for them, and re-layouts  6.09 us (3%)
    all_to_all x5, waiting for transfers between devices, exchange(): lax.all_to_all(parts.astype(WIRE), axis, 0, 0, tiled=True)  69.6 us
    all_to_all x5, starting transfers between devices, exchange(): lax.all_to_all(parts.astype(WIRE), axis, 0, 0, tiled=True)  23.5 us
    pallas_call x1, Pallas kernels, gradients(): pl.pallas_call(gradient_kernel, out_shape=(jax.ShapeDtypeStruct((parts, b...  19.6 us
    all_gather x1, waiting for transfers between devices, shards(): item_grad = lax.all_gather(item_own, 'user', axis=0, tiled=True)  11.7 us
    all_gather x1, waiting for transfers between devices, shards(): piece = lax.all_gather(user_factors, 'item', axis=1, tiled=True)  10.7 us
    pallas_call x1, Pallas kernels, variation(): pl.pallas_call(functools.partial(variation_kernel, group), out_shape=jax....  10.2 us
    convert_element_type x5, other arithmetic, exchange(): parts.astype(WIRE)  7.02 us
  transfers between devices with their start and end apart: 7, of which 6 were waited for; matrix products, arithmetic and copies ran while one was open for 3% of the time, Pallas kernels for 17%

profile of v4, /device:TPU:0, one launch (start us, length us, event | category | flops | bytes accessed | tf_op | source)
XLA Modules:
  0.0 176.4 jit_solution(5744301123414157623)
XLA Ops:
  7.2 0.0 all-gather.3.cloned.1.call-start
  7.2 0.7 all-gather.3.cloned.1.call-update
  7.9 0.0 copy-start.5
  7.9 0.0 copy-start.1
  7.9 2.8 %copy_bitcast_fusion.1 = f16[8,16,4,8,128]{4,3,2,1,0:T(8,128)(2,1)} fusion(f32[16,4,64,128]{3,2,1,0:T(8,128)} %param.13), kind=kLoop, calls=%fused_computation.5 | loop fusion | flops 524288 | bytes 3145728 | tf_op jit(solution)/shard_map/convert_element_type | solution.py:146
  10.7 7.3 %all-to-all-start = ((f16[8,16,4,8,128]{4,3,2,1,0:T(8,128)(2,1)}), f16[8,16,4,8,128]{4,3,2,1,0:T(8,128)(2,1)S(1)}, u32[]{:S(2)}, u32[]{:S(2)}) async-start(f16[8,16,4,8,128]{4,3,2,1,0:T(8,128)(2,1)} %copy_bitcast_fusion.1), calls=%async_computation | async-start | bytes 2097152 | tf_op jit(solution)/shard_map/all_to_all | solution.py:146
  18.0 0.0 copy-done.5
  18.0 0.1 copy.16
  18.1 0.1 broadcast_in_dim.3
  18.2 0.1 broadcast_in_dim_reshape.3.seen_ref
  18.3 10.7 %all-gather.3.cloned.1.call-done.piece_ref = bf16[16,256,128]{2,1,0:T(8,128)(2,1)} async-done(((bf16[16,64,128]{2,1,0:T(8,128)(2,1)}), bf16[16,256,128]{2,1,0:T(8,128)(2,1)}) %all-gather.3.cloned.1.call-update) | async-done | bytes 1048592 | tf_op jit(solution)/shard_map/all_gather | solution.py:156
  29.0 0.0 copy-done.1
  29.0 19.6 %shard_map.94 = (f32[4,16,64,128]{3,2,1,0:T(8,128)}, f32[2048,128]{1,0:T(8,128)S(1)}) custom-call(f32[16,1,2048]{2,1,0:T(1,128)S(1)} %broadcast_in_dim_reshape.3.seen_ref, bf16[16,256,128]{2,1,0:T(8,128)(2,1)} %all-gather.3.cloned.1.call-done.piece_ref, bf16[4096,2048]{1,0:T(8,128)(2,1)} %rating_ref.1, bf16[2048,128]{1,0:T(8,128)(2,1)S(1)} %copy-done.1), custom_call_target="tpu_custom_call" | custom-call | flops 25769803776 | bytes 16777216 | tf_op jit(solution)/shard_map/pallas_call | solution.py:48
  48.7 0.0 all-to-all-done
  48.7 0.0 copy-start.2
  48.7 1.7 bitcast_convert_fusion.dual_ref
  50.4 0.5 copy-done.2
  50.9 1.3 multiply_convert_fusion
  52.1 3.5 %all-to-all-start.1 = ((f16[4,16,64,128]{3,2,1,0:T(8,128)(2,1)}), f16[4,16,64,128]{3,2,1,0:T(8,128)(2,1)S(1)}, u32[]{:S(2)}, u32[]{:S(2)}) async-start(f16[4,16,64,128]{3,2,1,0:T(8,128)(2,1)} %multiply_convert_fusion), calls=%async_computation.1 | async-start | bytes 2097152 | tf_op jit(solution)/shard_map/all_to_all | solution.py:146
  55.7 0.9 multiply_convert_fusion.1
  56.6 13.5 %all-to-all-done.1 = f16[4,16,64,128]{3,2,1,0:T(8,128)(2,1)S(1)} async-done(((f16[4,16,64,128]{3,2,1,0:T(8,128)(2,1)}), f16[4,16,64,128]{3,2,1,0:T(8,128)(2,1)S(1)}, u32[]{:S(2)}, u32[]{:S(2)}) %all-to-all-start.1) | async-done | bytes 1048608 | tf_op jit(solution)/shard_map/all_to_all | solution.py:146
  70.1 5.5 %all-to-all-start.2 = ((f16[8,256,128]{2,1,0:T(8,128)(2,1)}), f16[8,256,128]{2,1,0:T(8,128)(2,1)S(1)}, u32[]{:S(2)}, u32[]{:S(2)}) async-start(f16[8,256,128]{2,1,0:T(8,128)(2,1)} %bitcast.3), calls=%async_computation.2 | async-start | bytes 1048576 | tf_op jit(solution)/shard_map/all_to_all | solution.py:146
  75.6 0.0 copy-start.4
  75.6 0.0 all-gather.5.cloned.1.call-start
  75.7 0.2 convert_reduce_fusion
  75.9 0.0 copy-start.6
  75.9 0.0 copy-start.7
  75.9 14.0 %all-to-all-done.2 = f16[8,256,128]{2,1,0:T(8,128)(2,1)S(1)} async-done(((f16[8,256,128]{2,1,0:T(8,128)(2,1)}), f16[8,256,128]{2,1,0:T(8,128)(2,1)S(1)}, u32[]{:S(2)}, u32[]{:S(2)}) %all-to-all-start.2) | async-done | bytes 524320 | tf_op jit(solution)/shard_map/all_to_all | solution.py:146
  89.9 0.1 convert_element_type.57
  90.0 0.7 reduce_sum.19
  90.7 0.0 all-gather.5.cloned.1.call-update
  90.7 0.0 copy-done.4
  90.7 0.8 copy_bitcast_fusion.2
  91.5 3.6 %all-to-all-start.3 = ((f16[8,16,8,128]{3,2,1,0:T(8,128)(2,1)}), f16[8,16,8,128]{3,2,1,0:T(8,128)(2,1)S(1)}, u32[]{:S(2)}, u32[]{:S(2)}) async-start(f16[8,16,8,128]{3,2,1,0:T(8,128)(2,1)} %copy_bitcast_fusion.2), calls=%async_computation.3 | async-start | bytes 524288 | tf_op jit(solution)/shard_map/all_to_all | solution.py:146
  95.2 0.0 copy-done.6
  95.2 0.1 copy.14
  95.3 0.1 reshape.37.near_ref
  95.4 0.0 copy-done.7
  95.4 0.1 copy.15
  95.5 0.1 reshape.38.weight_ref
  95.6 11.3 %all-to-all-done.3 = f16[8,16,8,128]{3,2,1,0:T(8,128)(2,1)S(1)} async-done(((f16[8,16,8,128]{3,2,1,0:T(8,128)(2,1)}), f16[8,16,8,128]{3,2,1,0:T(8,128)(2,1)S(1)}, u32[]{:S(2)}, u32[]{:S(2)}) %all-to-all-start.3) | async-done | bytes 262176 | tf_op jit(solution)/shard_map/all_to_all | solution.py:146
  106.9 0.1 bitcast_convert_fusion.1.target_ref
  107.0 0.0 copy-start
  107.0 1.6 copy-done
  108.6 10.2 %shard_map.95 = f32[128,5,8,128]{3,2,1,0:T(8,128)S(1)} custom-call(s32[512]{0:T(512)S(1)} %reshape.37.near_ref, f32[512]{0:T(512)S(1)} %reshape.38.weight_ref, f32[128,8,128]{2,1,0:T(8,128)S(1)} %bitcast_convert_fusion.1.target_ref, f32[128,4,8,128]{3,2,1,0:T(8,128)S(1)} %copy-done), custom_call_target="tpu_custom_call" | custom-call | flops 20971520 | bytes 4194304 | tf_op jit(solution)/shard_map/pallas_call | solution.py:120
  118.7 11.7 %all-gather.5.cloned.1.call-done = f32[2048,128]{1,0:T(8,128)} async-done(((f32[256,128]{1,0:T(8,128)}), f32[2048,128]{1,0:T(8,128)}) %all-gather.5.cloned.1.call-update) | async-done | bytes 1048592 | tf_op jit(solution)/shard_map/all_gather | solution.py:167
  130.4 1.2 convert_element_type.61
  131.6 3.6 %all-to-all-start.4 = ((f16[8,16,5,8,128]{4,3,2,1,0:T(8,128)(2,1)}), f16[8,16,5,8,128]{4,3,2,1,0:T(8,128)(2,1)S(1)}, u32[]{:S(2)}, u32[]{:S(2)}) async-start(f16[8,16,5,8,128]{4,3,2,1,0:T(8,128)(2,1)} %bitcast.25), calls=%async_computation.4 | async-start | bytes 2621440 | tf_op jit(solution)/shard_map/all_to_all | solution.py:146
  135.2 30.8 %all-to-all-done.4 = f16[8,16,5,8,128]{4,3,2,1,0:T(8,128)(2,1)S(1)} async-done(((f16[8,16,5,8,128]{4,3,2,1,0:T(8,128)(2,1)}), f16[8,16,5,8,128]{4,3,2,1,0:T(8,128)(2,1)S(1)}, u32[]{:S(2)}, u32[]{:S(2)}) %all-to-all-start.4) | async-done | bytes 1310752 | tf_op jit(solution)/shard_map/all_to_all | solution.py:146
  166.0 0.3 copy_bitcast_fusion
  166.3 0.0 copy-start.3
  166.3 1.5 slice.9
  167.8 0.8 slice_bitcast_fusion
  168.6 0.0 copy-done.3
  168.6 1.0 copy.24
  (1 shorter events, 0.0 us)
Async XLA Ops:
  7.2 21.9 %all-gather.3.cloned.1.call-start = ((), (), s32[]{:S(2)}) async-start(), calls=%async_computation.5 | async-start | bytes 1310720 | tf_op jit(solution)/shard_map/all_gather | solution.py:156
  7.9 10.1 %copy-start.5 = (s32[16,8]{0,1:T(8,128)S(1)}, s32[16,8]{0,1:T(8,128)}, u32[]{:S(2)}) copy-start(s32[16,8]{0,1:T(8,128)} %param.8) | copy-start | bytes 1540
  7.9 21.1 %copy-start.1 = (bf16[2048,128]{1,0:T(8,128)(2,1)S(1)}, bf16[2048,128]{1,0:T(8,128)(2,1)}, u32[]{:S(2)}) copy-start(bf16[2048,128]{1,0:T(8,128)(2,1)} %item_ref.1) | copy-start | bytes 1572868
  10.7 37.9 %all-to-all-start = ((f16[8,16,4,8,128]{4,3,2,1,0:T(8,128)(2,1)}), f16[8,16,4,8,128]{4,3,2,1,0:T(8,128)(2,1)S(1)}, u32[]{:S(2)}, u32[]{:S(2)}) async-start(f16[8,16,4,8,128]{4,3,2,1,0:T(8,128)(2,1)} %copy_bitcast_fusion.1), calls=%async_computation | async-start | bytes 2097152 | tf_op jit(solution)/shard_map/all_to_all | solution.py:146
  48.7 2.2 %copy-start.2 = (f32[4,16,64,128]{3,2,1,0:T(8,128)S(1)}, f32[4,16,64,128]{3,2,1,0:T(8,128)}, u32[]{:S(2)}) copy-start(f32[4,16,64,128]{3,2,1,0:T(8,128)} %get-tuple-element.14) | copy-start | bytes 6291460
  52.1 18.0 %all-to-all-start.1 = ((f16[4,16,64,128]{3,2,1,0:T(8,128)(2,1)}), f16[4,16,64,128]{3,2,1,0:T(8,128)(2,1)S(1)}, u32[]{:S(2)}, u32[]{:S(2)}) async-start(f16[4,16,64,128]{3,2,1,0:T(8,128)(2,1)} %multiply_convert_fusion), calls=%async_computation.1 | async-start | bytes 2097152 | tf_op jit(solution)/shard_map/all_to_all | solution.py:146
  70.1 19.8 %all-to-all-start.2 = ((f16[8,256,128]{2,1,0:T(8,128)(2,1)}), f16[8,256,128]{2,1,0:T(8,128)(2,1)S(1)}, u32[]{:S(2)}, u32[]{:S(2)}) async-start(f16[8,256,128]{2,1,0:T(8,128)(2,1)} %bitcast.3), calls=%async_computation.2 | async-start | bytes 1048576 | tf_op jit(solution)/shard_map/all_to_all | solution.py:146
  75.6 15.1 %copy-start.4 = (bf16[16,64,128]{2,1,0:T(8,128)(2,1)S(1)}, bf16[16,64,128]{2,1,0:T(8,128)(2,1)}, u32[]{:S(2)}) copy-start(bf16[16,64,128]{2,1,0:T(8,128)(2,1)} %param.9) | copy-start | bytes 786436
  75.6 54.8 %all-gather.5.cloned.1.call-start = ((), (), s32[]{:S(2)}) async-start(), calls=%async_computation.6 | async-start | bytes 1179648 | tf_op jit(solution)/shard_map/all_gather | solution.py:167
  75.9 19.2 %copy-start.6 = (s32[128,4]{0,1:T(4,128)S(1)}, s32[128,4]{0,1:T(4,128)}, u32[]{:S(2)}) copy-start(s32[128,4]{0,1:T(4,128)} %param.11) | copy-start | bytes 6148
  75.9 19.5 %copy-start.7 = (f32[128,4]{0,1:T(4,128)S(1)}, f32[128,4]{0,1:T(4,128)}, u32[]{:S(2)}) copy-start(f32[128,4]{0,1:T(4,128)} %param.12) | copy-start | bytes 6148
  91.5 15.4 %all-to-all-start.3 = ((f16[8,16,8,128]{3,2,1,0:T(8,128)(2,1)}), f16[8,16,8,128]{3,2,1,0:T(8,128)(2,1)S(1)}, u32[]{:S(2)}, u32[]{:S(2)}) async-start(f16[8,16,8,128]{3,2,1,0:T(8,128)(2,1)} %copy_bitcast_fusion.2), calls=%async_computation.3 | async-start | bytes 524288 | tf_op jit(solution)/shard_map/all_to_all | solution.py:146
  107.0 1.6 copy-start
  131.6 34.3 %all-to-all-start.4 = ((f16[8,16,5,8,128]{4,3,2,1,0:T(8,128)(2,1)}), f16[8,16,5,8,128]{4,3,2,1,0:T(8,128)(2,1)S(1)}, u32[]{:S(2)}, u32[]{:S(2)}) async-start(f16[8,16,5,8,128]{4,3,2,1,0:T(8,128)(2,1)} %bitcast.25), calls=%async_computation.4 | async-start | bytes 2621440 | tf_op jit(solution)/shard_map/all_to_all | solution.py:146
  166.3 2.3 %copy-start.3 = (f32[2048,128]{1,0:T(8,128)S(1)}, f32[2048,128]{1,0:T(8,128)}, u32[]{:S(2)}) copy-start(f32[2048,128]{1,0:T(8,128)} %all-gather.5.cloned.1.call-done) | copy-start | bytes 3145732
Sparse Core Ops, SparseCore 0:
  9.6 19.4 all-gather.2
  90.9 39.4 all-gather.4
